TPU v7x, 32 devices: a whole 2x2x4 slice. The times are simulated.
32 devices in a mesh: fsdp: 8 (over z, y), seq: 4 (over x, core).
Axes of the slice: x: 2, y: 2, z: 4, core: 2. Of those that a mesh axis runs over, the one named last changes fastest.
Arguments:
- inputs: bfloat16 [48, 512, 768], P('fsdp', 'seq'), may hold values from -6 to 6
- lengths: int32 [48], P('fsdp'), may hold values from 40 to 512, as said below
- w_query: bfloat16 [768, 768], P('fsdp'), may hold values from -0.3125 to 0.3125
- b_query: bfloat16 [768], P('fsdp'), may hold values from -3 to 3
- w_key: bfloat16 [768, 768], P('fsdp'), may hold values from -0.3125 to 0.3125
- w_value: bfloat16 [768, 768], P('fsdp'), may hold values from -0.21875 to 0.21875
- b_value: bfloat16 [768], P('fsdp'), may hold values from -3 to 3
- w_out: bfloat16 [768, 768], P('fsdp'), may hold values from -0.875 to 0.875
- b_out: bfloat16 [768], P('fsdp'), may hold values from -3 to 3
- gain_one: bfloat16 [768], P('fsdp'), may hold values from 0.5 to 1.5
- shift_one: bfloat16 [768], P('fsdp'), may hold values from -3 to 3
- w_inner: bfloat16 [768, 3072], P('fsdp'), may hold values from -0.21875 to 0.21875
- b_inner: bfloat16 [3072], P('fsdp'), may hold values from -3 to 3
- w_outer: bfloat16 [3072, 768], P('fsdp'), may hold values from -0.15625 to 0.15625
- b_outer: bfloat16 [768], P('fsdp'), may hold values from -3 to 3
- gain_two: bfloat16 [768], P('fsdp'), may hold values from 0.5 to 1.5
- shift_two: bfloat16 [768], P('fsdp'), may hold values from -3 to 3
- cotangent: bfloat16 [48, 512, 768], P('fsdp', 'seq'), may hold values from -6 to 6
Outputs:
- output: bfloat16 [48, 512, 768], P('fsdp', 'seq')
- grad_inputs: float32 [48, 512, 768], P('fsdp', 'seq')
- grad_w_query: float32 [768, 768], P('fsdp')
- grad_b_query: float32 [768], P('fsdp')
- grad_w_key: float32 [768, 768], P('fsdp')
- grad_w_value: float32 [768, 768], P('fsdp')
- grad_b_value: float32 [768], P('fsdp')
- grad_w_out: float32 [768, 768], P('fsdp')
- grad_b_out: float32 [768], P('fsdp')
- grad_gain_one: float32 [768], P('fsdp')
- grad_shift_one: float32 [768], P('fsdp')
- grad_w_inner: float32 [768, 3072], P('fsdp')
- grad_b_inner: float32 [3072], P('fsdp')
- grad_w_outer: float32 [3072, 768], P('fsdp')
- grad_b_outer: float32 [768], P('fsdp')
- grad_gain_two: float32 [768], P('fsdp')
- grad_shift_two: float32 [768], P('fsdp')
Inputs may be any that keep to these rules, and one draw needn't show every extreme that they name: `lengths`: real rows of each page; in every draw some page has exactly 512.
All inputs are finite; a program needn't handle non-finite values.
Results may differ from a plain program's by a relative error of at most 0.019.
Values may be sent and summed in bfloat16 or wider, within the bound.
A program may use at most 192 MiB of HBM per device.

v0:
```python
from functools import partial
import math

import jax
import jax.numpy as jnp
from jax import lax
from jax.sharding import PartitionSpec as P

HEADS = 12
HEAD_DIM = 64


negative_fill = -1e30
norm_eps = 1e-12


def matmul(left_side, right_side):
    return jnp.dot(left_side, right_side, preferred_element_type=jnp.float32)


def matmul_left_t(left_side, right_side):
    return lax.dot_general(
        left_side, right_side, (((0,), (0,)), ((), ())), preferred_element_type=jnp.float32
    )


def matmul_right_t(left_side, right_side):
    return lax.dot_general(
        left_side, right_side, (((1,), (1,)), ((), ())), preferred_element_type=jnp.float32
    )


def layer_norm(row_values, gain_vec, shift_vec):
    average = jnp.mean(row_values, -1, keepdims=True)
    centered = row_values - average
    spread = jnp.mean(centered * centered, -1, keepdims=True)
    return centered * lax.rsqrt(spread + norm_eps) * gain_vec + shift_vec


def masked_scores(query_rows, key_rows, length):
    head_scale = 1.0 / math.sqrt(HEAD_DIM)
    raw_scores = (
        jnp.einsum("rhd,khd->hrk", query_rows, key_rows, preferred_element_type=jnp.float32)
        * head_scale
    )
    key_valid = lax.broadcasted_iota(jnp.int32, raw_scores.shape, 2) < length
    return jnp.where(key_valid, raw_scores, negative_fill)


def attend_page(pieces):
    query_rows, key_rows, value_rows, length = pieces
    masked = masked_scores(query_rows, key_rows, length)
    row_top = jnp.max(masked, -1, keepdims=True)
    exp_scores = jnp.exp(masked - row_top)
    row_total = jnp.sum(exp_scores, -1, keepdims=True)
    attn_probs = exp_scores / row_total
    log_total = row_top[..., 0] + jnp.log(row_total[..., 0])
    context = jnp.einsum(
        "hrk,khd->rhd",
        attn_probs.astype(jnp.bfloat16),
        value_rows,
        preferred_element_type=jnp.float32,
    )
    return (context, log_total)


def attend_back(pieces):
    query_rows, key_rows, value_rows, length, log_total, grad_context = pieces
    head_scale = 1.0 / math.sqrt(HEAD_DIM)
    masked = masked_scores(query_rows, key_rows, length)
    attn_probs = jnp.exp(masked - log_total[..., None])
    grad_probs = jnp.einsum(
        "rhd,khd->hrk", grad_context, value_rows, preferred_element_type=jnp.float32
    )
    grad_values = jnp.einsum(
        "hrk,rhd->khd",
        attn_probs.astype(jnp.bfloat16),
        grad_context,
        preferred_element_type=jnp.float32,
    )
    row_delta = jnp.sum(attn_probs * grad_probs, -1, keepdims=True)
    grad_scores = (attn_probs * (grad_probs - row_delta)).astype(jnp.bfloat16)
    grad_query = (
        jnp.einsum("hrk,khd->rhd", grad_scores, key_rows, preferred_element_type=jnp.float32)
        * head_scale
    )
    grad_keys = (
        jnp.einsum("hrk,rhd->khd", grad_scores, query_rows, preferred_element_type=jnp.float32)
        * head_scale
    )
    return (grad_query, grad_keys, grad_values)


def forward_pass(inputs, lengths, attn_full, ffn_full):
    w_query, w_key, w_value, w_out, b_query, b_value, b_out, gain_one, shift_one = attn_full
    w_inner, w_outer, b_inner, b_outer, gain_two, shift_two = ffn_full
    page_count, row_count, feat_width = inputs.shape
    flat_in = inputs.reshape(page_count * row_count, feat_width)
    query_rows = (matmul(flat_in, w_query) + b_query.astype(jnp.float32)).astype(jnp.bfloat16)
    key_rows = matmul(flat_in, w_key).astype(jnp.bfloat16)
    value_rows = (matmul(flat_in, w_value) + b_value.astype(jnp.float32)).astype(jnp.bfloat16)
    keys_all, values_all = (
        lax.all_gather(
            key_rows.reshape(page_count, row_count, feat_width), "seq", axis=1, tiled=True
        ),
        lax.all_gather(
            value_rows.reshape(page_count, row_count, feat_width), "seq", axis=1, tiled=True
        ),
    )
    length_all = keys_all.shape[1]
    query_heads = query_rows.reshape(page_count, row_count, HEADS, HEAD_DIM)
    key_heads = keys_all.reshape(page_count, length_all, HEADS, HEAD_DIM)
    value_heads = values_all.reshape(page_count, length_all, HEADS, HEAD_DIM)
    context, log_total = lax.map(attend_page, (query_heads, key_heads, value_heads, lengths))
    context_low = context.reshape(page_count * row_count, feat_width).astype(jnp.bfloat16)
    attended = matmul(context_low, w_out) + b_out.astype(jnp.float32)
    mid_one = flat_in.astype(jnp.float32) + attended
    hidden_one = layer_norm(mid_one, gain_one.astype(jnp.float32), shift_one.astype(jnp.float32))
    hidden_low = hidden_one.astype(jnp.bfloat16)
    inner_pre = matmul(hidden_low, w_inner) + b_inner.astype(jnp.float32)
    activated = jax.nn.gelu(inner_pre, approximate=False).astype(jnp.bfloat16)
    outer_out = matmul(activated, w_outer) + b_outer.astype(jnp.float32)
    mid_two = hidden_one + outer_out
    layer_out = layer_norm(mid_two, gain_two.astype(jnp.float32), shift_two.astype(jnp.float32))
    return (
        query_heads,
        key_heads,
        value_heads,
        log_total,
        context_low,
        mid_one,
        hidden_low,
        inner_pre,
        activated,
        mid_two,
        layer_out,
    )


def per_device(
    inputs,
    lengths,
    w_query,
    b_query,
    w_key,
    w_value,
    b_value,
    w_out,
    b_out,
    gain_one,
    shift_one,
    w_inner,
    b_inner,
    w_outer,
    b_outer,
    gain_two,
    shift_two,
    cotangent,
):
    page_count, row_count, feat_width = inputs.shape
    attn_full = (
        lax.all_gather(w_query, "fsdp", axis=0, tiled=True),
        lax.all_gather(w_key, "fsdp", axis=0, tiled=True),
        lax.all_gather(w_value, "fsdp", axis=0, tiled=True),
        lax.all_gather(w_out, "fsdp", axis=0, tiled=True),
        lax.all_gather(b_query, "fsdp", axis=0, tiled=True),
        lax.all_gather(b_value, "fsdp", axis=0, tiled=True),
        lax.all_gather(b_out, "fsdp", axis=0, tiled=True),
        lax.all_gather(gain_one, "fsdp", axis=0, tiled=True),
        lax.all_gather(shift_one, "fsdp", axis=0, tiled=True),
    )
    ffn_full = (
        lax.all_gather(w_inner, "fsdp", axis=0, tiled=True),
        lax.all_gather(w_outer, "fsdp", axis=0, tiled=True),
        lax.all_gather(b_inner, "fsdp", axis=0, tiled=True),
        lax.all_gather(b_outer, "fsdp", axis=0, tiled=True),
        lax.all_gather(gain_two, "fsdp", axis=0, tiled=True),
        lax.all_gather(shift_two, "fsdp", axis=0, tiled=True),
    )
    forward_kept = forward_pass(inputs, lengths, attn_full, ffn_full)
    output = forward_kept[10].astype(jnp.bfloat16).reshape(page_count, row_count, feat_width)
    attn_back = (
        lax.all_gather(w_query, "fsdp", axis=0, tiled=True),
        lax.all_gather(w_key, "fsdp", axis=0, tiled=True),
        lax.all_gather(w_value, "fsdp", axis=0, tiled=True),
        lax.all_gather(w_out, "fsdp", axis=0, tiled=True),
        lax.all_gather(b_query, "fsdp", axis=0, tiled=True),
        lax.all_gather(b_value, "fsdp", axis=0, tiled=True),
        lax.all_gather(b_out, "fsdp", axis=0, tiled=True),
        lax.all_gather(gain_one, "fsdp", axis=0, tiled=True),
        lax.all_gather(shift_one, "fsdp", axis=0, tiled=True),
    )
    ffn_back = (
        lax.all_gather(w_inner, "fsdp", axis=0, tiled=True),
        lax.all_gather(w_outer, "fsdp", axis=0, tiled=True),
        lax.all_gather(b_inner, "fsdp", axis=0, tiled=True),
        lax.all_gather(b_outer, "fsdp", axis=0, tiled=True),
        lax.all_gather(gain_two, "fsdp", axis=0, tiled=True),
        lax.all_gather(shift_two, "fsdp", axis=0, tiled=True),
    )
    saved = forward_pass(inputs, lengths, attn_back, ffn_back)
    (
        query_heads,
        key_heads,
        value_heads,
        log_total,
        context_low,
        mid_one,
        hidden_low,
        inner_pre,
        activated,
        mid_two,
        unused_out,
    ) = saved
    (
        w_query_full,
        w_key_full,
        w_value_full,
        w_out_full,
        b_query_full,
        b_value_full,
        b_out_full,
        gain_one_full,
        shift_one_full,
    ) = attn_back
    w_inner_full, w_outer_full, b_inner_full, b_outer_full, gain_two_full, shift_two_full = ffn_back
    cot_flat = cotangent.reshape(page_count * row_count, feat_width).astype(jnp.float32)
    unused_two, second_pull = jax.vjp(
        layer_norm, mid_two, gain_two_full.astype(jnp.float32), shift_two_full.astype(jnp.float32)
    )
    grad_mid_two, grad_gain_two, grad_shift_two = second_pull(cot_flat)
    grad_outer = grad_mid_two.astype(jnp.bfloat16)
    grad_w_outer = matmul_left_t(activated, grad_outer)
    grad_b_outer = jnp.sum(grad_outer.astype(jnp.float32), 0)
    grad_activated = matmul_right_t(grad_outer, w_outer_full)
    unused_gelu, gelu_pull = jax.vjp(partial(jax.nn.gelu, approximate=False), inner_pre)
    grad_inner = gelu_pull(grad_activated)[0].astype(jnp.bfloat16)
    grad_w_inner = matmul_left_t(hidden_low, grad_inner)
    grad_b_inner = jnp.sum(grad_inner.astype(jnp.float32), 0)
    grad_hidden = grad_mid_two + matmul_right_t(grad_inner, w_inner_full)
    unused_one, first_pull = jax.vjp(
        layer_norm, mid_one, gain_one_full.astype(jnp.float32), shift_one_full.astype(jnp.float32)
    )
    grad_mid_one, grad_gain_one, grad_shift_one = first_pull(grad_hidden)
    grad_attended = grad_mid_one.astype(jnp.bfloat16)
    grad_w_out = matmul_left_t(context_low, grad_attended)
    grad_b_out = jnp.sum(grad_attended.astype(jnp.float32), 0)
    grad_context = (
        matmul_right_t(grad_attended, w_out_full)
        .astype(jnp.bfloat16)
        .reshape(page_count, row_count, HEADS, HEAD_DIM)
    )
    grad_query, grad_keys_all, grad_values_all = lax.map(
        attend_back, (query_heads, key_heads, value_heads, lengths, log_total, grad_context)
    )
    length_all = grad_keys_all.shape[1]
    grad_keys_own, grad_values_own = (
        lax.psum_scatter(
            grad_keys_all.reshape(page_count, length_all, feat_width).astype(jnp.bfloat16),
            "seq",
            scatter_dimension=1,
            tiled=True,
        ).astype(jnp.float32),
        lax.psum_scatter(
            grad_values_all.reshape(page_count, length_all, feat_width).astype(jnp.bfloat16),
            "seq",
            scatter_dimension=1,
            tiled=True,
        ).astype(jnp.float32),
    )
    grad_query_low = grad_query.reshape(page_count * row_count, feat_width).astype(jnp.bfloat16)
    grad_keys_low = grad_keys_own.reshape(page_count * row_count, feat_width).astype(jnp.bfloat16)
    grad_values_low = grad_values_own.reshape(page_count * row_count, feat_width).astype(
        jnp.bfloat16
    )
    flat_in = inputs.reshape(page_count * row_count, feat_width)
    grad_w_query = matmul_left_t(flat_in, grad_query_low)
    grad_b_query = jnp.sum(grad_query_low.astype(jnp.float32), 0)
    grad_w_key = matmul_left_t(flat_in, grad_keys_low)
    grad_w_value = matmul_left_t(flat_in, grad_values_low)
    grad_b_value = jnp.sum(grad_values_low.astype(jnp.float32), 0)
    grad_inputs = (
        grad_mid_one
        + matmul_right_t(grad_query_low, w_query_full)
        + matmul_right_t(grad_keys_low, w_key_full)
        + matmul_right_t(grad_values_low, w_value_full)
    )
    part_w_inner, part_w_outer, part_b_inner, part_b_outer, part_gain_two, part_shift_two = (
        lax.psum_scatter(grad_w_inner, "fsdp", scatter_dimension=0, tiled=True),
        lax.psum_scatter(grad_w_outer, "fsdp", scatter_dimension=0, tiled=True),
        lax.psum_scatter(grad_b_inner, "fsdp", scatter_dimension=0, tiled=True),
        lax.psum_scatter(grad_b_outer, "fsdp", scatter_dimension=0, tiled=True),
        lax.psum_scatter(grad_gain_two, "fsdp", scatter_dimension=0, tiled=True),
        lax.psum_scatter(grad_shift_two, "fsdp", scatter_dimension=0, tiled=True),
    )
    (
        part_w_query,
        part_w_key,
        part_w_value,
        part_w_out,
        part_b_query,
        part_b_value,
        part_b_out,
        part_gain_one,
        part_shift_one,
    ) = (
        lax.psum_scatter(grad_w_query, "fsdp", scatter_dimension=0, tiled=True),
        lax.psum_scatter(grad_w_key, "fsdp", scatter_dimension=0, tiled=True),
        lax.psum_scatter(grad_w_value, "fsdp", scatter_dimension=0, tiled=True),
        lax.psum_scatter(grad_w_out, "fsdp", scatter_dimension=0, tiled=True),
        lax.psum_scatter(grad_b_query, "fsdp", scatter_dimension=0, tiled=True),
        lax.psum_scatter(grad_b_value, "fsdp", scatter_dimension=0, tiled=True),
        lax.psum_scatter(grad_b_out, "fsdp", scatter_dimension=0, tiled=True),
        lax.psum_scatter(grad_gain_one, "fsdp", scatter_dimension=0, tiled=True),
        lax.psum_scatter(grad_shift_one, "fsdp", scatter_dimension=0, tiled=True),
    )
    totals = (
        lax.psum(part_w_query.astype(jnp.bfloat16), "seq").astype(jnp.float32),
        lax.psum(part_b_query.astype(jnp.bfloat16), "seq").astype(jnp.float32),
        lax.psum(part_w_key.astype(jnp.bfloat16), "seq").astype(jnp.float32),
        lax.psum(part_w_value.astype(jnp.bfloat16), "seq").astype(jnp.float32),
        lax.psum(part_b_value.astype(jnp.bfloat16), "seq").astype(jnp.float32),
        lax.psum(part_w_out.astype(jnp.bfloat16), "seq").astype(jnp.float32),
        lax.psum(part_b_out.astype(jnp.bfloat16), "seq").astype(jnp.float32),
        lax.psum(part_gain_one.astype(jnp.bfloat16), "seq").astype(jnp.float32),
        lax.psum(part_shift_one.astype(jnp.bfloat16), "seq").astype(jnp.float32),
        lax.psum(part_w_inner.astype(jnp.bfloat16), "seq").astype(jnp.float32),
        lax.psum(part_b_inner.astype(jnp.bfloat16), "seq").astype(jnp.float32),
        lax.psum(part_w_outer.astype(jnp.bfloat16), "seq").astype(jnp.float32),
        lax.psum(part_b_outer.astype(jnp.bfloat16), "seq").astype(jnp.float32),
        lax.psum(part_gain_two.astype(jnp.bfloat16), "seq").astype(jnp.float32),
        lax.psum(part_shift_two.astype(jnp.bfloat16), "seq").astype(jnp.float32),
    )
    (
        total_w_query,
        total_b_query,
        total_w_key,
        total_w_value,
        total_b_value,
        total_w_out,
        total_b_out,
        total_gain_one,
        total_shift_one,
        total_w_inner,
        total_b_inner,
        total_w_outer,
        total_b_outer,
        total_gain_two,
        total_shift_two,
    ) = totals
    return (
        output,
        grad_inputs.reshape(page_count, row_count, feat_width),
        total_w_query,
        total_b_query,
        total_w_key,
        total_w_value,
        total_b_value,
        total_w_out,
        total_b_out,
        total_gain_one,
        total_shift_one,
        total_w_inner,
        total_b_inner,
        total_w_outer,
        total_b_outer,
        total_gain_two,
        total_shift_two,
    )


def solution(mesh):
    return jax.shard_map(
        per_device,
        mesh=mesh,
        in_specs=(
            P("fsdp", "seq", None),
            P("fsdp"),
            P("fsdp", None),
            P("fsdp"),
            P("fsdp", None),
            P("fsdp", None),
            P("fsdp"),
            P("fsdp", None),
            P("fsdp"),
            P("fsdp"),
            P("fsdp"),
            P("fsdp", None),
            P("fsdp"),
            P("fsdp", None),
            P("fsdp"),
            P("fsdp"),
            P("fsdp"),
            P("fsdp", "seq", None),
        ),
        out_specs=(
            P("fsdp", "seq", None),
            P("fsdp", "seq", None),
            P("fsdp", None),
            P("fsdp"),
            P("fsdp", None),
            P("fsdp", None),
            P("fsdp"),
            P("fsdp", None),
            P("fsdp"),
            P("fsdp"),
            P("fsdp"),
            P("fsdp", None),
            P("fsdp"),
            P("fsdp", None),
            P("fsdp"),
            P("fsdp"),
            P("fsdp"),
        ),
        check_vma=False,
    )
```

profile of v0, /device:TPU:0, one launch (start us, length us, event | category | flops | bytes accessed | tf_op | source)
XLA Modules:
  0.0 1456.4 jit_solution(602530092829682446)
XLA Ops:
  18.1 39.1 %all-reduce.18 = (bf16[768]{0:T(1024)(128)(2,1)S(1)}, bf16[768]{0:T(1024)(128)(2,1)S(1)}, bf16[768]{0:T(1024)(128)(2,1)S(1)}, bf16[768]{0:T(1024)(128)(2,1)S(1)}...) all-reduce(bf16[768]{0:T(1024)(128)(2,1)S(1)} %dynamic-update-slice, ...), channel_id=1, replica_groups=mesh['fsdp'=8,'seq'=4] {'fsdp'}, use_global_device_ids=true, to_apply=%add.1 | all-reduce | flops 6144 | bytes 24576
  57.2 3.8 add_convert_fusion.3
  61.1 35.1 %all-gather.16.cloned.1.call-done = bf16[768,768]{1,0:T(8,128)(2,1)} async-done(((bf16[96,768]{1,0:T(8,128)(2,1)}), bf16[768,768]{1,0:T(8,128)(2,1)}) %all-gather.16.cloned.1.call-update) | async-done | bytes 1179664 | tf_op jit(solution)/shard_map/all_gather | solution.py:163
  96.3 3.4 convolution_convert_fusion.1
  102.5 26.1 %all-gather = bf16[8,1,384]{2,1,0:T(2,128)(2,1)S(1)} all-gather(bf16[1,1,384]{2,1,0:T(2,128)(2,1)S(1)} %reshape.239), channel_id=1, replica_groups=mesh['fsdp'=8,'seq'=4] {'fsdp'}, dimensions={0}, use_global_device_ids=true | all-gather | bytes 6912 | tf_op jit(solution)/shard_map/all_gather | solution.py:175
  130.4 7.8 all-gather.14.cloned.1.call-done
  140.6 3.3 reshape.280
  143.8 4.0 copy.81
  147.8 28.6 %all-gather.12.cloned.1.call-done = bf16[6,512,768]{2,1,0:T(8,128)(2,1)} async-done(((bf16[6,128,768]{2,1,0:T(8,128)(2,1)}), bf16[6,512,768]{2,1,0:T(8,128)(2,1)}) %all-gather.12.cloned.1.call-update) | async-done | bytes 4718608 | tf_op jit(solution)/shard_map/all_gather | solution.py:106
  176.4 6.7 copy.78
  183.2 32.8 %all-gather.18.cloned.1.call-done = bf16[6,512,768]{2,1,0:T(8,128)(2,1)} async-done(((bf16[6,128,768]{2,1,0:T(8,128)(2,1)}), bf16[6,512,768]{2,1,0:T(8,128)(2,1)}) %all-gather.18.cloned.1.call-update) | async-done | bytes 4718608 | tf_op jit(solution)/shard_map/all_gather | solution.py:103
  215.9 6.7 copy.80
  222.9 36.2 %while.36 = (s32[]{:T(128)}, bf16[6,128,12,64]{1,3,2,0:T(8,128)(2,1)S(1)}, bf16[6,512,12,64]{1,3,2,0:T(8,128)(2,1)}, s32[6]{0:T(128)S(1)}, bf16[6,128,12,64]{1,3...) while((s32[]{:T(128)}, bf16[6,128,12,64]{1,3,2,0:T(8,128)(2,1)S(1)}, ...), condition=%wide.region_3.4_spmd, body=%wide.region_0.3_spmd.sunk | while | flops 207619072 | bytes 14763101 | solution.py:114
  261.2 3.1 fusion.149
  266.6 73.3 %all-gather.22.cloned.1.call-done = bf16[768,3072]{1,0:T(8,128)(2,1)} async-done(((bf16[96,3072]{1,0:T(8,128)(2,1)}), bf16[768,3072]{1,0:T(8,128)(2,1)}) %all-gather.22.cloned.1.call-update) | async-done | bytes 4718608 | tf_op jit(solution)/shard_map/all_gather | solution.py:173
  340.0 80.2 %all-gather.24.cloned.1.call-done = bf16[3072,768]{1,0:T(8,128)(2,1)} async-done(((bf16[384,768]{1,0:T(8,128)(2,1)}), bf16[3072,768]{1,0:T(8,128)(2,1)}) %all-gather.24.cloned.1.call-update) | async-done | bytes 4718608 | tf_op jit(solution)/shard_map/all_gather | solution.py:174
  420.2 31.8 %fusion.150 = (f32[768]{0:T(1024)S(1)}, f32[768,768]{1,0:T(8,128)S(1)}) fusion(f32[768]{0:T(1024)} %convert_element_type.266, bf16[3072,768]{1,0:T(8,128)(2,1)} %all-gather.24.cloned.1.call-done, bf16[768,3072]{1,0:T(8,128)(2,1)} %all-gather.22.cloned.1.call-done, f32[3072]{0:T(1024)} %bitcast.264, f32[768,768]{1,0:T(8,128)} %copy-done.7, ...), kind=kOutput, calls=%fused_computation.231 | convolution fusion | flops 7410547712 | bytes 14186496 | tf_op jit(solution)/shard_map/dot_general | solution.py:18
  454.0 48.8 %while.37 = (s32[]{:T(128)}, bf16[6,128,12,64]{1,3,2,0:T(8,128)(2,1)}, f32[6,12,128]{2,1,0:T(8,128)}, bf16[6,512,12,64]{1,3,2,0:T(8,128)(2,1)}, s32[6]{0:T(128)}...) while((s32[]{:T(128)}, bf16[6,128,12,64]{1,3,2,0:T(8,128)(2,1)}, ...), condition=%wide.region_11.12_spmd, body=%wide.region_8.11_spmd.sunk | while | flops 210762752 | bytes 11655781 | solution.py:114
  459.2 2.9 fusion.219
  467.3 2.9 fusion.219
  475.5 2.9 fusion.219
  483.6 2.9 fusion.219
  491.8 2.9 fusion.219
  499.9 2.9 fusion.219
  508.9 26.9 %multiply_convert_fusion.1 = (bf16[768,3072]{1,0:T(8,128)(2,1)S(1)}, f32[768,3072]{1,0:T(8,128)}, f32[768,3072]{1,0:T(8,128)}) fusion(f32[3072]{0:T(1024)S(1)} %bitcast.265, bf16[768,3072]{1,0:T(8,128)(2,1)S(1)} %bitcast.268, f32[768,768]{1,0:T(8,128)S(1)} %get-tuple-element.412, f32[768]{0:T(1024)S(1)} %fusion.106, f32[768]{0:T(1024)S(1)} %broadcast_multiply_fusion.1, ...), kind=kOutput, calls=%fused_computation.84 | convolution fusion | flops 3782541312 | bytes 30695424 | tf_op jit(solution)/shard_map/dot_general | solution.py:18
  535.8 4.1 fusion.148
  545.9 12.9 convert_reduce_fusion
  558.8 9.2 multiply_reduce_fusion.1
  573.6 4.7 reshape.260
  578.3 4.5 copy.87
  584.1 74.9 %while.38 = (s32[]{:T(128)}, bf16[6,128,12,64]{1,3,2,0:T(8,128)(2,1)}, bf16[6,512,12,64]{1,3,2,0:T(8,128)(2,1)}, bf16[6,512,12,64]{1,3,2,0:T(8,128)(2,1)}, bf16[...) while((s32[]{:T(128)}, ...), condition=%wide.region_22.23_spmd, body=%wide.region_20.22_spmd.sunk | while | flops 510884864 | bytes 30316796 | solution.py:253
  594.1 2.5 fusion.229
  619.1 2.5 fusion.229
  631.6 2.5 fusion.229
  659.0 8.7 copy.96
  667.8 6.3 copy.113
  674.1 9.5 copy.98
  683.6 6.4 copy.114
  691.3 4.2 fusion.89
  699.0 2.5 convolution_bitcast_fusion.2
  701.5 3.1 copy.100
  704.6 15.5 %reduce-scatter.25.cloned.1.call-done = bf16[128,4608]{1,0:T(8,128)(2,1)} async-done(((bf16[512,4608]{1,0:T(8,128)(2,1)}), bf16[128,4608]{1,0:T(8,128)(2,1)}) %reduce-scatter.25.cloned.1.call-update) | async-done | bytes 1179664
  720.2 3.6 reshape.262
  726.4 2.5 convolution_bitcast_fusion.1
  728.9 3.2 copy.102
  732.2 38.4 %reduce-scatter.27.cloned.1.call-done = bf16[128,4608]{1,0:T(8,128)(2,1)} async-done(((bf16[512,4608]{1,0:T(8,128)(2,1)}), bf16[128,4608]{1,0:T(8,128)(2,1)}) %reduce-scatter.27.cloned.1.call-update) | async-done | bytes 1179664
  770.6 3.6 reshape.264
  776.2 4.2 convolution_bitcast_fusion
  780.4 3.3 copy.104
  783.9 10.9 fusion.138
  796.1 8.8 fusion.154
  808.7 4.3 fusion.87
  813.0 30.3 %reduce-scatter.19.cloned.1.call-done = f32[96,768]{1,0:T(8,128)} async-done(((f32[768,768]{1,0:T(8,128)}), f32[96,768]{1,0:T(8,128)}) %reduce-scatter.19.cloned.1.call-update) | async-done | bytes 294928 | tf_op jit(solution)/shard_map/reduce_scatter | solution.py:310
  844.9 69.8 %reduce-scatter.29.cloned.1.call-done = f32[96,768]{1,0:T(8,128)} async-done(((f32[768,768]{1,0:T(8,128)}), f32[96,768]{1,0:T(8,128)}) %reduce-scatter.29.cloned.1.call-update) | async-done | bytes 294928
  916.6 2.6 copy.90
  919.4 36.2 %all-reduce.17 = (bf16[768]{0:T(1024)(128)(2,1)S(1)}, bf16[768]{0:T(1024)(128)(2,1)S(1)}, bf16[768]{0:T(1024)(128)(2,1)S(1)}, bf16[768]{0:T(1024)(128)(2,1)S(1)}...) all-reduce(f32[768]{0:T(1024)} %reduce_sum.240, ...), channel_id=5, replica_groups=mesh['fsdp'=8,'seq'=4] {'fsdp'}, use_global_device_ids=true, to_apply=%region_28.29.clone | all-reduce | flops 9216 | bytes 55296
  956.3 5.7 all-reduce.19
  966.7 20.2 %reduce-scatter.31.cloned.1.call-done = f32[96,768]{1,0:T(8,128)} async-done(((f32[768,768]{1,0:T(8,128)}), f32[96,768]{1,0:T(8,128)}) %reduce-scatter.31.cloned.1.call-update) | async-done | bytes 294928
  988.7 69.7 %reduce-scatter.33.cloned.1.call-done = f32[96,768]{1,0:T(8,128)} async-done(((f32[768,768]{1,0:T(8,128)}), f32[96,768]{1,0:T(8,128)}) %reduce-scatter.33.cloned.1.call-update) | async-done | bytes 294928
  1060.2 164.1 %reduce-scatter.21.cloned.1.call-done = f32[96,3072]{1,0:T(8,128)} async-done(((f32[768,3072]{1,0:T(8,128)}), f32[96,3072]{1,0:T(8,128)}) %reduce-scatter.21.cloned.1.call-update) | async-done | bytes 1179664 | tf_op jit(solution)/shard_map/reduce_scatter | solution.py:289
  1226.4 163.7 %reduce-scatter.23.cloned.1.call-done = f32[384,768]{1,0:T(8,128)} async-done(((f32[3072,768]{1,0:T(8,128)}), f32[384,768]{1,0:T(8,128)}) %reduce-scatter.23.cloned.1.call-update) | async-done | bytes 1179664 | tf_op jit(solution)/shard_map/reduce_scatter | solution.py:290
  1392.3 2.5 fusion.153
  1395.0 2.7 add_add_fusion.2
  1397.7 44.3 %all-reduce.23.cloned.1.call-done = (bf16[96,768]{0,1:T(8,128)(2,1)}, bf16[96,768]{0,1:T(8,128)(2,1)}, bf16[96,768]{0,1:T(8,128)(2,1)}, bf16[96,768]{1,0:T(8,128...) async-done(((bf16[96,768]{0,1:T(8,128)(2,1)}, bf16[96,768]{0,1:T(8,128)(2,1)}, bf16[96,768]{0,1:T(8,128)(2,1)}, bf16[96,768]{1,0:T(8,128)(2,1)}, ...) | async-done | bytes 1769488 | tf_op jit(solution)/shard_map/psum | solution.py:318
  (346 shorter events, 215.3 us)
Async XLA Ops:
  7.2 50.1 %all-gather.10.cloned.1.call-start = ((), (), s32[]{:S(2)}) async-start(), calls=%async_computation.8 | async-start | bytes 1327104 | tf_op jit(solution)/shard_map/all_gather | solution.py:164
  7.9 88.3 %all-gather.16.cloned.1.call-start = ((), (), s32[]{:S(2)}) async-start(), calls=%async_computation.11 | async-start | bytes 1327104 | tf_op jit(solution)/shard_map/all_gather | solution.py:163
  8.7 129.5 %all-gather.14.cloned.1.call-start = ((), (), s32[]{:S(2)}) async-start(), calls=%async_computation.10 | async-start | bytes 1327104 | tf_op jit(solution)/shard_map/all_gather | solution.py:162
  9.4 167.0 %all-gather.12.cloned.1.call-start = ((), (), s32[]{:S(2)}) async-start(), calls=%async_computation.9 | async-start | bytes 5898240 | tf_op jit(solution)/shard_map/all_gather | solution.py:106
  57.2 39.0 %copy-start.34 = (bf16[6,128,768]{2,1,0:T(8,128)(2,1)S(1)}, bf16[6,128,768]{2,1,0:T(8,128)(2,1)}, u32[]{:S(2)}) copy-start(bf16[6,128,768]{2,1,0:T(8,128)(2,1)} %param.24) | copy-start | bytes 3538948
  61.1 154.8 %all-gather.18.cloned.1.call-start = ((), (), s32[]{:S(2)}) async-start(), calls=%async_computation.12 | async-start | bytes 5898240 | tf_op jit(solution)/shard_map/all_gather | solution.py:103
  99.6 2.8 copy-start.33
  99.7 161.5 %all-gather.20.cloned.1.call-start = ((), (), s32[]{:S(2)}) async-start(), calls=%async_computation.13 | async-start | bytes 1327104 | tf_op jit(solution)/shard_map/all_gather | solution.py:165
  100.3 239.7 %all-gather.22.cloned.1.call-start = ((), (), s32[]{:S(2)}) async-start(), calls=%async_computation.14 | async-start | bytes 5308416 | tf_op jit(solution)/shard_map/all_gather | solution.py:173
  101.0 319.2 %all-gather.24.cloned.1.call-start = ((), (), s32[]{:S(2)}) async-start(), calls=%async_computation.15 | async-start | bytes 5308416 | tf_op jit(solution)/shard_map/all_gather | solution.py:174
  101.7 618.4 %reduce-scatter.25.cloned.1.call-start = ((), (), s32[]{:S(2)}) async-start(), calls=%async_computation.19 | async-start | bytes 5898240
  101.8 159.3 %copy-start.31 = (f32[768]{0:T(1024)}, f32[768]{0:T(1024)S(1)}, u32[]{:S(2)}) copy-start(f32[768]{0:T(1024)S(1)} %convert_element_type.260) | copy-start | bytes 9220
  183.2 39.7 %copy-start.39 = (s32[6]{0:T(128)S(1)}, s32[6]{0:T(128)}, u32[]{:S(2)}) copy-start(s32[6]{0:T(128)} %param.25) | copy-start | bytes 76
  259.1 2.1 copy-start.35
  264.2 1.4 copy-start.7
  502.8 2.3 copy-start.32
  502.8 2.4 copy-start.36
  502.8 2.4 copy-start.38
  505.1 1.4 copy-start.9
  505.1 3.6 slice-start
  505.2 3.7 slice-start.1
  505.2 30.6 %slice-start.2 = ((s8[4718592]{0:T(1024)(128)(4,1)}), s8[4194304]{0:T(1024)(128)(4,1)S(1)}, s32[]{:S(2)}) async-start(s8[4718592]{0:T(1024)(128)(4,1)} %bitcast.269), calls=%async_computation.27 | async-start | bytes 8388608
  506.5 61.6 %copy-start = (f32[768,768]{1,0:T(8,128)}, f32[768,768]{1,0:T(8,128)S(1)}, u32[]{:S(2)}) copy-start(f32[768,768]{1,0:T(8,128)S(1)} %get-tuple-element.412) | copy-start | bytes 7077892
  506.5 2.4 copy-start.29
  508.9 26.9 %copy-start.30 = (f32[768]{0:T(1024)S(1)}, f32[768]{0:T(1024)}, u32[]{:S(2)}) copy-start(f32[768]{0:T(1024)} %convert_element_type.266) | copy-start | bytes 9220
  508.9 26.9 %slice-start.3 = ((s8[4718592]{0:T(1024)(128)(4,1)}), s8[524288]{0:T(1024)(128)(4,1)S(1)}, s32[]{:S(2)}) async-start(s8[4718592]{0:T(1024)(128)(4,1)} %bitcast.269), calls=%async_computation.28 | async-start | bytes 1048576
  535.8 4.2 copy-start.41
  540.0 1.3 copy-start.1
  540.0 1.3 copy-start.25
  541.2 1.5 copy-start.26
  545.9 12.9 copy-start.11
  558.8 9.2 copy-start.5
  584.1 2.6 copy-start.40
  596.6 2.6 copy-start.40
  609.1 2.6 copy-start.40
  621.6 2.6 copy-start.40
  634.0 2.6 copy-start.40
  646.5 2.6 copy-start.40
  674.0 96.5 %reduce-scatter.27.cloned.1.call-start = ((), (), s32[]{:S(2)}) async-start(), calls=%async_computation.20 | async-start | bytes 5898240
  690.0 1.3 copy-start.14
  690.1 153.2 %reduce-scatter.19.cloned.1.call-start = ((), (), s32[]{:S(2)}) async-start(), calls=%async_computation.16 | async-start | bytes 2654208 | tf_op jit(solution)/shard_map/reduce_scatter | solution.py:310
  695.5 3.5 copy-start.37
  695.5 219.2 %reduce-scatter.29.cloned.1.call-start = ((), (), s32[]{:S(2)}) async-start(), calls=%async_computation.21 | async-start | bytes 2654208
  697.8 1.1 copy-start.10
  704.6 282.3 %reduce-scatter.31.cloned.1.call-start = ((), (), s32[]{:S(2)}) async-start(), calls=%async_computation.22 | async-start | bytes 2654208
  732.1 326.2 %reduce-scatter.33.cloned.1.call-start = ((), (), s32[]{:S(2)}) async-start(), calls=%async_computation.23 | async-start | bytes 2654208
  776.2 4.2 copy-start.3
  783.7 440.6 %reduce-scatter.21.cloned.1.call-start = ((), (), s32[]{:S(2)}) async-start(), calls=%async_computation.17 | async-start | bytes 10616832 | tf_op jit(solution)/shard_map/reduce_scatter | solution.py:289
  794.8 1.3 copy-start.12
  794.8 595.3 %reduce-scatter.23.cloned.1.call-start = ((), (), s32[]{:S(2)}) async-start(), calls=%async_computation.18 | async-start | bytes 10616832 | tf_op jit(solution)/shard_map/reduce_scatter | solution.py:290
  804.9 1.5 copy-start.2
  804.9 637.1 %all-reduce.23.cloned.1.call-start = ((), (), s32[]{:S(2)}) async-start(), calls=%async_computation.24 | async-start | bytes 3833856 | tf_op jit(solution)/shard_map/psum | solution.py:318
  813.0 106.2 %copy-start.4 = (bf16[6,128,768]{1,2,0:T(8,128)(2,1)S(1)}, bf16[6,128,768]{1,2,0:T(8,128)(2,1)}, u32[]{:S(2)}) copy-start(bf16[6,128,768]{1,2,0:T(8,128)(2,1)} %copy-done.3) | copy-start | bytes 3538948
  813.0 106.4 %copy-start.27 = (f32[768]{0:T(1024)S(1)}, f32[768]{0:T(1024)}, u32[]{:S(2)}) copy-start(f32[768]{0:T(1024)} %get-tuple-element.390) | copy-start | bytes 9220
  813.0 106.4 %copy-start.28 = (f32[768]{0:T(1024)S(1)}, f32[768]{0:T(1024)}, u32[]{:S(2)}) copy-start(f32[768]{0:T(1024)} %get-tuple-element.394) | copy-start | bytes 9220
  1060.2 332.1 %copy-start.17 = (bf16[6,128,768]{2,1,0:T(8,128)(2,1)S(1)}, bf16[6,128,768]{2,1,0:T(8,128)(2,1)}, u32[]{:S(2)}) copy-start(bf16[6,128,768]{2,1,0:T(8,128)(2,1)} %copy-done.16) | copy-start | bytes 3538948
  1392.3 2.6 copy-start.6
  1392.3 2.6 copy-start.8
  1392.3 2.7 copy-start.15
  1392.3 2.7 copy-start.23
  1442.0 4.4 copy-start.21
  1442.0 5.1 copy-start.20
  1442.0 6.0 copy-start.19
  1442.0 6.9 copy-start.18
  (4 other events, 3.3 us)
Sparse Core Ops, SparseCore 0:
  10.2 43.9 all-gather.9
  56.4 39.8 all-gather.15
  98.5 39.7 all-gather.13
  140.2 36.2 all-gather.11
  178.4 37.4 all-gather.17
  218.0 41.0 all-gather.19
  261.3 78.6 all-gather.21
  342.2 78.0 all-gather.23
  674.2 45.9 reduce-scatter.24
  722.7 47.8 reduce-scatter.26
  774.1 69.1 reduce-scatter.18
  846.7 68.0 reduce-scatter.28
  918.3 68.5 reduce-scatter.30
  990.3 68.0 reduce-scatter.32
  1061.8 162.3 reduce-scatter.20
  1227.7 162.3 reduce-scatter.22
  1393.3 48.6 all-reduce.22
where the time goes:
time: 1470 us; the launch traced here: 1460 us
  waiting for transfers between devices  878 us (60%)
  matrix products  255 us (17%)
  local copies, waits for them, and re-layouts  139 us (9%)
  blocking collectives  107 us (7%)
  other arithmetic  58.4 us (4%)
  between operations  16.8 us (1%)
    unnamed x22, waiting for transfers between devices  218 us
    reduce_scatter x1, waiting for transfers between devices, per_device(): lax.psum_scatter(grad_w_inner, 'fsdp', scatter_dimension=0, tiled=True)  164 us
    reduce_scatter x1, waiting for transfers between devices, per_device(): lax.psum_scatter(grad_w_outer, 'fsdp', scatter_dimension=0, tiled=True)  164 us
    unnamed x135, local copies, waits for them, and re-layouts  80.6 us
    all_gather x1, waiting for transfers between devices, per_device(): lax.all_gather(w_outer, 'fsdp', axis=0, tiled=True)  80.2 us
    dot_general x8, matrix products, matmul(): return jnp.dot(left_side, right_side, preferred_element_type=jnp.float32)  76.7 us
    unnamed x2, blocking collectives  75.3 us
    all_gather x1, waiting for transfers between devices, per_device(): lax.all_gather(w_inner, 'fsdp', axis=0, tiled=True)  73.3 us
  transfers between devices with their start and end apart: 17, of which 15 were waited for; matrix products, arithmetic and copies ran while one was open for 13% of the time, Pallas kernels for 0%

commit v1 on v0

v1 whole, which is shorter than its diff:
```python
import functools
import math

import jax
import jax.numpy as jnp
from jax import lax
from jax.experimental import pallas as pl
from jax.experimental.pallas import tpu as pltpu
from jax.sharding import PartitionSpec as P

HEADS = 12
HEAD_DIM = 64
PAIR = 2 * HEAD_DIM
NEG = -1e30
EPS = 1e-12
BF = jnp.bfloat16
F32 = jnp.float32
MESH = pl.DeviceIdType.MESH
ANY = pl.BlockSpec(memory_space=pl.ANY)
VM = pl.BlockSpec(memory_space=pltpu.VMEM)
CHUNK = 512
ROW = 96
VMEM_CAP = 60 << 20

NN = (((1,), (0,)), ((), ()))
NT = (((1,), (1,)), ((), ()))
TN = (((0,), (0,)), ((), ()))


def dot(a, b, dims=NN):
    return lax.dot_general(a, b, dims, preferred_element_type=F32)


def call(body, cost, **kw):
    flops, byts, trans = cost
    params = dict(vmem_limit_bytes=VMEM_CAP)
    params.update(kw.pop("params", {}))
    return pl.pallas_call(
        body,
        compiler_params=pltpu.CompilerParams(**params),
        cost_estimate=pl.CostEstimate(
            flops=int(flops), bytes_accessed=int(byts), transcendentals=int(trans)
        ),
        **kw,
    )


def attn_fwd_body(thr, xa, xb, xc, xd, wq, wk, wv, vec, q_o, k_o, v_o, p_o, c_o, bias):
    page = pl.program_id(0)
    x_all = jnp.concatenate([xa[0], xb[0], xc[0], xd[0]], axis=0)
    own = x_all.shape[0] // 2
    query = (dot(x_all[:own], wq[...]) + vec[0:1, :]).astype(BF)
    q_o[0] = query
    k_o[0] = dot(x_all, wk[...]).astype(BF)
    v_o[0] = (dot(x_all, wv[...]) + vec[1:2, :]).astype(BF)
    blk = xa.shape[1]
    place = lax.broadcasted_iota(jnp.int32, (blk, own), 0)
    for b in range(4):
        bias[b * blk : (b + 1) * blk, :] = jnp.where(place < thr[page, b], 0.0, NEG)
    low_lane = lax.broadcasted_iota(jnp.int32, (own, PAIR), 1) < HEAD_DIM

    def pair(i, carry):
        cols = pl.ds(pl.multiple_of(i * PAIR, PAIR), PAIR)
        qp = q_o[0, :, cols] * jnp.array(1.0 / math.sqrt(HEAD_DIM), BF)
        kp = k_o[0, :, cols]
        vt = v_o[0, :, cols].T
        outs = []
        for h in range(2):
            keep = low_lane if h == 0 else jnp.logical_not(low_lane)
            qh = jnp.where(keep, qp, jnp.zeros_like(qp))
            st = dot(kp, qh, NT) + bias[...]
            top = jnp.max(st, axis=0, keepdims=True)
            ex = jnp.exp(st - top)
            tot = jnp.sum(ex, axis=0, keepdims=True)
            pt = (ex * (1.0 / tot)).astype(BF)
            p_o[0, 2 * i + h] = pt
            outs.append(dot(vt[h * HEAD_DIM : (h + 1) * HEAD_DIM], pt))
        c_o[0, :, cols] = jnp.concatenate(outs, axis=0).T.astype(BF)
        return carry

    lax.fori_loop(0, HEADS // 2, pair, 0)


def attn_fwd(thr, xs, wq, wk, wv, vec):
    pages, blk, d = xs[0].shape
    own, rows = 2 * blk, 4 * blk
    const = lambda p, t: (0, 0)
    by_page = lambda p, t: (p, 0, 0)
    one = pl.Buffered(1)
    return call(
        attn_fwd_body,
        (
            pages * (2 * d * d * (own + 2 * rows) + 4 * own * rows * d),
            pages * rows * d * 2 * 4 + 6 * d * d + pages * HEADS * own * rows * 2,
            pages * HEADS * own * rows,
        ),
        grid_spec=pltpu.PrefetchScalarGridSpec(
            num_scalar_prefetch=1,
            grid=(pages,),
            in_specs=[pl.BlockSpec((1, blk, d), by_page)] * 4
            + [pl.BlockSpec((d, d), const, pipeline_mode=one)] * 3
            + [pl.BlockSpec((8, d), const)],
            out_specs=[
                pl.BlockSpec((1, own, d), by_page),
                pl.BlockSpec((1, rows, d), by_page),
                pl.BlockSpec((1, rows, d), by_page),
                pl.BlockSpec((1, HEADS, rows, own), lambda p, t: (p, 0, 0, 0)),
                pl.BlockSpec((1, own, d), by_page),
            ],
            scratch_shapes=[pltpu.VMEM((rows, own), F32)],
        ),
        out_shape=[
            jax.ShapeDtypeStruct((pages, own, d), BF),
            jax.ShapeDtypeStruct((pages, rows, d), BF),
            jax.ShapeDtypeStruct((pages, rows, d), BF),
            jax.ShapeDtypeStruct((pages, HEADS, rows, own), BF),
            jax.ShapeDtypeStruct((pages, own, d), BF),
        ],
        name="attn_fwd",
    )(thr, *xs, wq, wk, wv, vec)


def attn_bwd_body(q, k, v, p, ctx, dctx, dq_o, dk_own, dk_oth, dv_own, dv_oth):
    own = q.shape[1]
    low_lane = lax.broadcasted_iota(jnp.int32, (own, PAIR), 1) < HEAD_DIM
    scale = 1.0 / math.sqrt(HEAD_DIM)

    def pair(i, carry):
        cols = pl.ds(pl.multiple_of(i * PAIR, PAIR), PAIR)
        qp = q[0, :, cols] * jnp.array(scale, BF)
        kp = k[0, :, cols]
        kt = kp.T
        vp = v[0, :, cols]
        dc = dctx[0, :, cols]
        prod = (dc.astype(F32) * ctx[0, :, cols].astype(F32)).T
        dk = None
        dv = None
        dqs = []
        for h in range(2):
            keep = low_lane if h == 0 else jnp.logical_not(low_lane)
            feats = slice(h * HEAD_DIM, (h + 1) * HEAD_DIM)
            dch = jnp.where(keep, dc, jnp.zeros_like(dc))
            qh = jnp.where(keep, qp, jnp.zeros_like(qp))
            pt = p[0, 2 * i + h]
            delta = jnp.sum(prod[feats], axis=0, keepdims=True)
            dpt = dot(vp, dch, NT)
            dst = (pt.astype(F32) * (dpt - delta)).astype(BF)
            dvh = dot(pt, dch)
            dkh = dot(dst, qh)
            dk = dkh if dk is None else dk + dkh
            dv = dvh if dv is None else dv + dvh
            dqs.append(dot(kt[feats], dst))
        dq_o[0, :, cols] = (jnp.concatenate(dqs, axis=0) * scale).T.astype(BF)
        dk_own[0, :, cols] = dk[:own].astype(BF)
        dk_oth[0, :, cols] = dk[own:].astype(BF)
        dv_own[0, :, cols] = dv[:own].astype(BF)
        dv_oth[0, :, cols] = dv[own:].astype(BF)
        return carry

    lax.fori_loop(0, HEADS // 2, pair, 0)


def attn_bwd(q, k, v, p, ctx, dctx):
    pages, own, d = q.shape
    rows = k.shape[1]
    by_page = lambda i: (i, 0, 0)
    o = pl.BlockSpec((1, own, d), by_page)
    r = pl.BlockSpec((1, rows, d), by_page)
    return call(
        attn_bwd_body,
        (pages * 10 * own * rows * d, pages * (own * rows * HEADS * 2 + 10 * own * d * 2), 0),
        grid=(pages,),
        in_specs=[o, r, r, pl.BlockSpec((1, HEADS, rows, own), lambda i: (i, 0, 0, 0)), o, o],
        out_specs=[o] * 5,
        out_shape=[jax.ShapeDtypeStruct((pages, own, d), BF)] * 5,
        name="attn_bwd",
    )(q, k, v, p, ctx, dctx)


def normal_parts(v):
    bell = jnp.exp(v * v * -0.5)
    t = 1.0 / (1.0 + jnp.abs(v) * (0.3275911 / math.sqrt(2.0)))
    tail = t * (
        0.127414796 + t * (-0.142248368 + t * (0.7107068705 + t * (-0.7265760135 + t * 0.5307027145)))
    )
    tail = tail * bell
    return jnp.where(v >= 0.0, 1.0 - tail, tail), bell * (1.0 / math.sqrt(2.0 * math.pi))


def row_norm(v):
    centered = v - jnp.mean(v, -1, keepdims=True)
    inv = lax.rsqrt(jnp.mean(centered * centered, -1, keepdims=True) + EPS)
    return centered * inv, inv


def norm_back(e, n, inv):
    return inv * (e - jnp.mean(e, -1, keepdims=True) - n * jnp.mean(e * n, -1, keepdims=True))


def ffn_body(
    ctx, xa, xb, ca, cb, wo, wi, w2, vec, b_in,
    out_a, out_b, gm1_o, dctx_o, dwo_o, dwi_o, dw2_o, gvec, gbin,
    act, din, dgel, hid, gout, gatt, ctx_all,
):
    page = pl.program_id(0)
    blk = xa.shape[1]
    own = 2 * blk
    ff = wi.shape[1]
    here = pl.ds(pl.multiple_of(page * own, own), own)

    @pl.when(page == 0)
    def _():
        gvec[...] = jnp.zeros_like(gvec)
        gbin[...] = jnp.zeros_like(gbin)

    ctx_v = ctx[0]
    ctx_all[here, :] = ctx_v
    x_own = jnp.concatenate([xa[0], xb[0]], axis=0).astype(F32)
    mid_one = x_own + (dot(ctx_v, wo[...]) + vec[2:3, :])
    n1, r1 = row_norm(mid_one)
    h1 = n1 * vec[3:4, :] + vec[4:5, :]
    hl = h1.astype(BF)
    hid[here, :] = hl

    def up(j, acc):
        cols = pl.ds(pl.multiple_of(j * CHUNK, CHUNK), CHUNK)
        pre = dot(hl, wi[:, cols]) + b_in[:, cols]
        big, bell = normal_parts(pre)
        a = (pre * big).astype(BF)
        dgel[:, cols] = (big + pre * bell).astype(BF)
        act[here, cols] = a
        return acc + dot(a, w2[cols, :])

    outer = lax.fori_loop(0, ff // CHUNK, up, jnp.zeros((own, x_own.shape[1]), F32))
    mid_two = h1 + (outer + vec[5:6, :])
    n2, r2 = row_norm(mid_two)
    res = (n2 * vec[6:7, :] + vec[7:8, :]).astype(BF)
    out_a[0] = res[:blk]
    out_b[0] = res[blk:]
    cot = jnp.concatenate([ca[0], cb[0]], axis=0).astype(F32)
    gm2 = norm_back(cot * vec[6:7, :], n2, r2)
    go = gm2.astype(BF)
    gout[here, :] = go

    def down(j, acc):
        cols = pl.ds(pl.multiple_of(j * CHUNK, CHUNK), CHUNK)
        di = (dot(go, w2[cols, :], NT) * dgel[:, cols].astype(F32)).astype(BF)
        din[here, cols] = di
        gbin[:, cols] += jnp.sum(di.astype(F32), 0, keepdims=True)
        return acc + dot(di, wi[:, cols], NT)

    gh = gm2 + lax.fori_loop(0, ff // CHUNK, down, jnp.zeros_like(gm2))
    gm1 = norm_back(gh * vec[3:4, :], n1, r1)
    gm1_o[0] = gm1
    ga = gm1.astype(BF)
    gatt[here, :] = ga
    dctx_o[0] = dot(ga, wo[...], NT).astype(BF)

    def add(row, value):
        gvec[row : row + 1, :] += jnp.sum(value, 0, keepdims=True)

    add(2, ga.astype(F32))
    add(3, gh * n1)
    add(4, gh)
    add(5, go.astype(F32))
    add(6, cot * n2)
    add(7, cot)

    @pl.when(page == pl.num_programs(0) - 1)
    def _():
        go_all = gout[...]
        hid_t = hid[...].T

        def grads(j, carry):
            cols = pl.ds(pl.multiple_of(j * CHUNK, CHUNK), CHUNK)
            dw2_o[cols, :] = dot(act[:, cols], go_all, TN).astype(BF)
            dwi_o[:, cols] = dot(hid_t, din[:, cols]).astype(BF)
            return carry

        lax.fori_loop(0, ff // CHUNK, grads, 0)
        dwo_o[...] = dot(ctx_all[...], gatt[...], TN).astype(BF)


def ffn(ctx, xa, xb, ca, cb, wo, wi, w2, vec, b_in):
    pages, own, d = ctx.shape
    blk = own // 2
    ff = wi.shape[1]
    n = pages * own
    by_page = lambda p: (p, 0, 0)
    const = lambda p: (0, 0)
    one = pl.Buffered(1)
    half = pl.BlockSpec((1, blk, d), by_page)
    whole = pl.BlockSpec((1, own, d), by_page)

    def fixed(*shape):
        return pl.BlockSpec(shape, const, pipeline_mode=one)

    return call(
        ffn_body,
        (n * d * (12 * ff + 6 * d), 4 * d * ff * 2 + 12 * n * d * 2, n * ff),
        grid=(pages,),
        in_specs=[whole, half, half, half, half, fixed(d, d), fixed(d, ff), fixed(ff, d), fixed(8, d), fixed(1, ff)],
        out_specs=[half, half, whole, whole, fixed(d, d), fixed(d, ff), fixed(ff, d), fixed(8, d), fixed(1, ff)],
        out_shape=[
            jax.ShapeDtypeStruct((pages, blk, d), BF),
            jax.ShapeDtypeStruct((pages, blk, d), BF),
            jax.ShapeDtypeStruct((pages, own, d), F32),
            jax.ShapeDtypeStruct((pages, own, d), BF),
            jax.ShapeDtypeStruct((d, d), BF),
            jax.ShapeDtypeStruct((d, ff), BF),
            jax.ShapeDtypeStruct((ff, d), BF),
            jax.ShapeDtypeStruct((8, d), F32),
            jax.ShapeDtypeStruct((1, ff), F32),
        ],
        scratch_shapes=[
            pltpu.VMEM((n, ff), BF),
            pltpu.VMEM((n, ff), BF),
            pltpu.VMEM((own, ff), BF),
            pltpu.VMEM((n, d), BF),
            pltpu.VMEM((n, d), BF),
            pltpu.VMEM((n, d), BF),
            pltpu.VMEM((n, d), BF),
        ],
        name="ffn",
    )(ctx, xa, xb, ca, cb, wo, wi, w2, vec, b_in)


def proj_body(
    xa, xb, dq, dk, dkr, dv, dvr, gm1, wq, wk, wv,
    ga_o, gb_o, dwq_o, dwk_o, dwv_o, gvec, x_all, dq_all, dk_all, dv_all,
):
    page = pl.program_id(0)
    blk = xa.shape[1]
    own = 2 * blk
    here = pl.ds(pl.multiple_of(page * own, own), own)
    x_all[here, :] = jnp.concatenate([xa[0], xb[0]], axis=0)
    dq_v = dq[0]
    dk_v = (dk[0].astype(F32) + dkr[0].astype(F32)).astype(BF)
    dv_v = (dv[0].astype(F32) + dvr[0].astype(F32)).astype(BF)
    dq_all[here, :] = dq_v
    dk_all[here, :] = dk_v
    dv_all[here, :] = dv_v
    gx = gm1[0] + dot(dq_v, wq[...], NT) + dot(dk_v, wk[...], NT) + dot(dv_v, wv[...], NT)
    ga_o[0] = gx[:blk]
    gb_o[0] = gx[blk:].astype(BF)

    @pl.when(page == 0)
    def _():
        gvec[...] = jnp.zeros_like(gvec)

    gvec[0:1, :] += jnp.sum(dq_v.astype(F32), 0, keepdims=True)
    gvec[1:2, :] += jnp.sum(dv_v.astype(F32), 0, keepdims=True)

    @pl.when(page == pl.num_programs(0) - 1)
    def _():
        x_t = x_all[...].T
        dwq_o[...] = dot(x_t, dq_all[...]).astype(BF)
        dwk_o[...] = dot(x_t, dk_all[...]).astype(BF)
        dwv_o[...] = dot(x_t, dv_all[...]).astype(BF)


def proj(xa, xb, dq, dk, dkr, dv, dvr, gm1, wq, wk, wv):
    pages, own, d = dq.shape
    blk = own // 2
    n = pages * own
    by_page = lambda p: (p, 0, 0)
    const = lambda p: (0, 0)
    one = pl.Buffered(1)
    half = pl.BlockSpec((1, blk, d), by_page)
    whole = pl.BlockSpec((1, own, d), by_page)
    square = pl.BlockSpec((d, d), const, pipeline_mode=one)
    return call(
        proj_body,
        (12 * n * d * d, 12 * d * d + 16 * n * d, 0),
        grid=(pages,),
        in_specs=[half, half] + [whole] * 6 + [square] * 3,
        out_specs=[half, half] + [square] * 3 + [pl.BlockSpec((8, d), const)],
        out_shape=[
            jax.ShapeDtypeStruct((pages, blk, d), F32),
            jax.ShapeDtypeStruct((pages, blk, d), BF),
        ]
        + [jax.ShapeDtypeStruct((d, d), BF)] * 3
        + [jax.ShapeDtypeStruct((8, d), F32)],
        scratch_shapes=[pltpu.VMEM((n, d), BF)] * 4,
        name="proj_bwd",
    )(xa, xb, dq, dk, dkr, dv, dvr, gm1, wq, wk, wv)


def place():
    f, s = lax.axis_index("fsdp"), lax.axis_index("seq")
    return lax.div(f, 2), lax.rem(f, 2), lax.div(s, 2), lax.rem(s, 2)


def at(z, y, x, c):
    return {"fsdp": 2 * z + y, "seq": 2 * x + c}


def meet(others):
    barrier = pltpu.get_barrier_semaphore()
    for other in others:
        pl.semaphore_signal(barrier, inc=1, device_id=other, device_id_type=MESH)
    pl.semaphore_wait(barrier, len(others))


def remote(src, dst, send, recv, other):
    copy = pltpu.make_async_remote_copy(
        src_ref=src, dst_ref=dst, send_sem=send, recv_sem=recv,
        device_id=other, device_id_type=MESH,
    )
    copy.start()
    return copy


def neighbours(z, y, x, c):
    n_z = 4
    zs = [at(lax.rem(z + k, n_z), y, x, c) for k in range(1, n_z)]
    far = [at(lax.rem(z + k, n_z), 1 - y, x, c) for k in range(n_z)]
    return zs + far + [at(z, y, 1 - x, c), at(z, y, x, 1 - c)]


def piece_views(wq, wk, wv, wo, wi, w2, lead):
    views = []

    def add(ref, row0, col0):
        def view(sel, rows, cols):
            r0, nr = rows
            c0, nc = cols
            r = pl.ds(row0 + r0, nr)
            c = pl.ds(col0 + c0, nc)
            return ref.at[sel + (r, c)] if lead else ref.at[r, c]

        views.append(view)

    for ref in (wq, wk, wv, wo):
        add(ref, 0, 0)
    for j in range(4):
        add(wi, 0, 768 * j)
    for j in range(4):
        add(w2, ROW * j, 0)
    return views


ALL = slice(None)


def gather_body(
    x_in, cot, wq, wk, wv, wo, wi, w2, vec,
    gq, gk, gv, go, gi, g2, xa, xb, xc, xd, ca, cb, gvec,
    lsem, zs, zr, ys, yr, xs, xr, cs, cr, asend, arecv, aloc, vs, vr,
):
    z, y, x, c = place()
    f = 2 * z + y
    meet(neighbours(z, y, x, c))
    x_peer, c_peer, y_peer = at(z, y, 1 - x, c), at(z, y, x, 1 - c), at(z, 1 - y, x, c)
    own_pages, sent_pages = pl.ds(3 * x, 3), pl.ds(3 * (1 - x), 3)
    src = piece_views(wq, wk, wv, wo, wi, w2, False)
    dst = piece_views(gq, gk, gv, go, gi, g2, True)
    n = len(src)
    half_cols = (pl.multiple_of(c * 384, 128), 384)
    full = (0, ROW)
    mine = (pl.multiple_of(x * (ROW // 2), 16), ROW // 2)
    wide = [p % 2 == 0 for p in range(n)]

    to_b = remote(x_in.at[sent_pages], xb, asend.at[0], arecv.at[0], x_peer)
    to_c = remote(x_in.at[own_pages], xc, asend.at[1], arecv.at[1], c_peer)
    locals_ = [
        pltpu.make_async_copy(x_in.at[own_pages], xa, aloc.at[0]),
        pltpu.make_async_copy(cot.at[own_pages], ca, aloc.at[1]),
        pltpu.make_async_copy(vec, gvec.at[f], aloc.at[2]),
    ]
    for copy in locals_:
        copy.start()
    vecs = [
        remote(vec, gvec.at[f], vs.at[k], vr.at[k], {"fsdp": lax.rem(f + k + 1, 8)})
        for k in range(7)
    ]
    own = [
        pltpu.make_async_copy(
            src[p]((), full if wide[p] else mine, half_cols),
            dst[p]((z, y), full if wide[p] else mine, half_cols),
            lsem.at[p],
        )
        for p in range(n)
    ]
    for copy in own:
        copy.start()
    along_z, along_y, along_x, along_c = [], [], [], []
    to_d = None
    to_cb = None
    for t in range(n + 3):
        if t < n:
            rows = full if wide[t] else mine
            along_z.append(
                [
                    remote(
                        src[t]((), rows, half_cols), dst[t]((z, y), rows, half_cols),
                        zs.at[t, k], zr.at[t, k], at(lax.rem(z + k + 1, 4), y, x, c),
                    )
                    for k in range(3)
                ]
            )
        p = t - 1
        if 0 <= p < n:
            own[p].wait()
            for copy in along_z[p]:
                copy.wait_recv()
            view = dst[p]((ALL, y), mine, half_cols)
            along_y.append(remote(view, view, ys.at[p], yr.at[p], y_peer))
        p = t - 2
        if 0 <= p < n:
            along_y[p].wait_recv()
            view = dst[p]((ALL, 1 - y) if wide[p] else (ALL, ALL), mine, half_cols)
            along_x.append(remote(view, view, xs.at[p], xr.at[p], x_peer))
        p = t - 3
        if 0 <= p < n:
            along_x[p].wait_recv()
            view = dst[p]((ALL, ALL), full, half_cols)
            along_c.append(remote(view, view, cs.at[p], cr.at[p], c_peer))
        if t == 2:
            to_b.wait_recv()
            to_d = remote(xb, xd, asend.at[2], arecv.at[2], c_peer)
            to_cb = remote(cot.at[sent_pages], cb, asend.at[3], arecv.at[3], x_peer)
    for copy in along_c:
        copy.wait_recv()
    to_c.wait_recv()
    to_d.wait_recv()
    to_cb.wait_recv()
    for copy in vecs:
        copy.wait_recv()
    for group in along_z:
        for copy in group:
            copy.wait_send()
    for copy in along_y + along_x + along_c + vecs + [to_b, to_c, to_d, to_cb]:
        copy.wait_send()
    for copy in locals_:
        copy.wait()


def gather_all(x_in, cot, ws, vec):
    half = jax.ShapeDtypeStruct((3,) + x_in.shape[1:], BF)
    dma = pltpu.SemaphoreType.DMA
    n = 12
    outs = [jax.ShapeDtypeStruct((4, 2) + w.shape, BF) for w in ws]
    res = call(
        gather_body,
        (0, sum(16 * w.size for w in ws), 0),
        in_specs=[ANY] * 9,
        out_specs=[ANY] * 13,
        out_shape=outs + [half] * 6 + [jax.ShapeDtypeStruct((8,) + vec.shape, vec.dtype)],
        scratch_shapes=[
            dma((n,)), dma((n, 3)), dma((n, 3)), dma((n,)), dma((n,)), dma((n,)), dma((n,)),
            dma((n,)), dma((n,)), dma((4,)), dma((4,)), dma((3,)), dma((7,)), dma((7,)),
        ],
        params=dict(collective_id=0, has_side_effects=True),
        name="gather_all",
    )(x_in, cot, *ws, vec)
    full = [r.reshape(-1, r.shape[-1]) for r in res[:6]]
    return full, res[6:10], res[10:12], res[12]


def scatter_body(
    gq, gk, gv, go, gi, g2, out_a, out_b, gx_a, gx_b, gvec,
    oq, ok, ov, oo, oi, o2, out, gx, ovec,
    acc, rc, rx, ry, rz, fin, rf, rgx, vecin, vtot, vx,
    lsem, cs, cr, xs, xr, ys, yr, zs, zr, fs, fr, es, er, asend, arecv, aloc, vs, vr, us, ur,
):
    z, y, x, c = place()
    f = 2 * z + y
    meet(neighbours(z, y, x, c) + [at(z, y, 1 - x, 1 - c)])
    x_peer, c_peer, y_peer = at(z, y, 1 - x, c), at(z, y, x, 1 - c), at(z, 1 - y, x, c)
    own_pages = pl.ds(3 * x, 3)
    other_pages = pl.ds(3 * (1 - x), 3)
    src = piece_views(gq, gk, gv, go, gi, g2, True)
    dst = piece_views(oq, ok, ov, oo, oi, o2, False)
    n = len(src)
    hr = ROW // 2
    half_cols = (pl.multiple_of(c * 384, 128), 384)
    their_cols = (pl.multiple_of((1 - c) * 384, 128), 384)
    full = (0, ROW)
    mine = pl.ds(pl.multiple_of(x * hr, 16), hr)
    theirs = pl.ds(pl.multiple_of((1 - x) * hr, 16), hr)
    wide = [p % 2 == 0 for p in range(n)]

    back_x = remote(gx_b, rgx, asend.at[0], arecv.at[0], x_peer)
    vecs = []
    for k in range(7):
        to = lax.rem(f + k + 1, 8)
        vecs.append(remote(gvec.at[to], vecin.at[k], vs.at[k], vr.at[k], {"fsdp": to}))
    keep_out = pltpu.make_async_copy(out_a, out.at[own_pages], aloc.at[0])
    keep_out.start()
    mine_first = []
    to_core = []
    for p in range(n):
        copy = pltpu.make_async_copy(src[p]((ALL, ALL), full, half_cols), acc.at[p], lsem.at[p])
        copy.start()
        mine_first.append(copy)
        to_core.append(
            remote(src[p]((ALL, ALL), full, their_cols), rc.at[p], cs.at[p], cr.at[p], c_peer)
        )
    back_out = remote(out_b, out.at[own_pages], asend.at[1], arecv.at[1], x_peer)

    gx[own_pages] = gx_a[...]
    along_x, along_y, along_z, finals, ends = [], [], [], [], []
    vec_x = []
    for t in range(n + 5):
        p = t
        if p < n:
            mine_first[p].wait()
            to_core[p].wait_recv()
            acc[p] = (acc[p].astype(F32) + rc[p].astype(F32)).astype(BF)
            if wide[p]:
                along_x.append(
                    remote(acc.at[p, :, 1 - y, theirs, :], rx.at[p, :, 0], xs.at[p], xr.at[p], x_peer)
                )
            else:
                along_x.append(
                    remote(acc.at[p, :, :, theirs, :], rx.at[p], xs.at[p], xr.at[p], x_peer)
                )
        p = t - 1
        if 0 <= p < n:
            along_x[p].wait_recv()
            if wide[p]:
                acc[p, :, 1 - y, mine, :] = (
                    acc[p, :, 1 - y, mine, :].astype(F32) + rx[p, :, 0].astype(F32)
                ).astype(BF)
            else:
                acc[p, :, :, mine, :] = (
                    acc[p, :, :, mine, :].astype(F32) + rx[p].astype(F32)
                ).astype(BF)
            along_y.append(
                remote(acc.at[p, :, 1 - y, mine, :], ry.at[p], ys.at[p], yr.at[p], y_peer)
            )
        p = t - 2
        if 0 <= p < n:
            along_y[p].wait_recv()
            acc[p, :, y, mine, :] = (
                acc[p, :, y, mine, :].astype(F32) + ry[p].astype(F32)
            ).astype(BF)
            group = []
            for k in range(3):
                to = lax.rem(z + k + 1, 4)
                if wide[p]:
                    a, b = acc.at[p, to, y], rz.at[p, k]
                else:
                    a, b = acc.at[p, to, y, mine, :], rz.at[p, k, pl.ds(0, hr)]
                group.append(remote(a, b, zs.at[p, k], zr.at[p, k], at(to, y, x, c)))
            along_z.append(group)
        p = t - 3
        if 0 <= p < n:
            for copy in along_z[p]:
                copy.wait_recv()
            if wide[p]:
                total = acc[p, z, y].astype(F32)
                for k in range(3):
                    total = total + rz[p, k].astype(F32)
                fin[p] = total.astype(BF)
                finals.append(remote(fin.at[p], rf.at[p], fs.at[p], fr.at[p], x_peer))
            else:
                total = acc[p, z, y, mine, :].astype(F32)
                for k in range(3):
                    total = total + rz[p, k, :hr].astype(F32)
                fin[p, :hr] = total.astype(BF)
                finals.append(
                    remote(fin.at[p, pl.ds(0, hr)], rf.at[p, pl.ds(0, hr)], fs.at[p], fr.at[p], x_peer)
                )
        p = t - 4
        if 0 <= p < n:
            finals[p].wait_recv()
            if wide[p]:
                dst[p]((), full, half_cols)[...] = fin[p].astype(F32) + rf[p].astype(F32)
            else:
                dst[p]((), (pl.multiple_of(x * hr, 16), hr), half_cols)[...] = fin[p, :hr].astype(F32)
                dst[p]((), (pl.multiple_of((1 - x) * hr, 16), hr), half_cols)[...] = rf[p, :hr].astype(F32)
            view = dst[p]((), full, half_cols)
            ends.append(remote(view, view, es.at[p], er.at[p], c_peer))
        if t == 1:
            total = gvec[f]
            for copy in vecs:
                copy.wait_recv()
            for k in range(7):
                total = total + vecin[k]
            vtot[...] = total
            vec_x = [
                remote(vtot, vx.at[0], us.at[0], ur.at[0], x_peer),
            ]
        if t == 3:
            vec_x[0].wait_recv()
            vx[1] = vtot[...] + vx[0]
            vec_x.append(remote(vx.at[1], vx.at[2], us.at[1], ur.at[1], c_peer))
        if t == 5:
            back_x.wait_recv()
            gx[other_pages] = rgx[...].astype(F32)
    vec_x[1].wait_recv()
    ovec[...] = vx[1] + vx[2]
    for copy in ends:
        copy.wait_recv()
    back_out.wait_recv()
    keep_out.wait()
    for group in along_z:
        for copy in group:
            copy.wait_send()
    for copy in to_core + along_x + along_y + finals + ends + vecs + vec_x + [back_x, back_out]:
        copy.wait_send()


def scatter_all(grads, out_a, out_b, gx_a, gx_b, gvec, shards):
    dma = pltpu.SemaphoreType.DMA
    n = 12
    pages, blk, d = out_a.shape
    views = [g.reshape((4, 2) + shape) for g, shape in zip(grads, shards)]
    vmem = pltpu.VMEM
    res = call(
        scatter_body,
        (0, sum(16 * g.size for g in grads), 0),
        in_specs=[ANY] * 6 + [ANY, ANY, VM, ANY, VM],
        out_specs=[VM] * 6 + [ANY, VM, VM],
        out_shape=[jax.ShapeDtypeStruct(shape, F32) for shape in shards]
        + [
            jax.ShapeDtypeStruct((2 * pages, blk, d), BF),
            jax.ShapeDtypeStruct((2 * pages, blk, d), F32),
            jax.ShapeDtypeStruct(gvec.shape[1:], F32),
        ],
        scratch_shapes=[
            vmem((n, 4, 2, ROW, 384), BF),
            vmem((n, 4, 2, ROW, 384), BF),
            vmem((n, 4, 2, ROW // 2, 384), BF),
            vmem((n, 4, ROW // 2, 384), BF),
            vmem((n, 3, ROW, 384), BF),
            vmem((n, ROW, 384), BF),
            vmem((n, ROW, 384), BF),
            vmem((pages, blk, d), BF),
            vmem((7,) + gvec.shape[1:], F32),
            vmem(gvec.shape[1:], F32),
            vmem((3,) + gvec.shape[1:], F32),
            dma((n,)), dma((n,)), dma((n,)), dma((n,)), dma((n,)), dma((n,)), dma((n,)),
            dma((n, 3)), dma((n, 3)), dma((n,)), dma((n,)), dma((n,)), dma((n,)),
            dma((2,)), dma((2,)), dma((1,)), dma((7,)), dma((7,)), dma((2,)), dma((2,)),
        ],
        params=dict(collective_id=1, has_side_effects=True),
        name="scatter_all",
    )(*views, out_a, out_b, gx_a, gx_b, gvec)
    return res[:6], res[6], res[7], res[8]


SWAP_X = [(0, 2), (2, 0), (1, 3), (3, 1)]
SWAP_C = [(0, 1), (1, 0), (2, 3), (3, 2)]


def swap(value, pairs):
    return lax.ppermute(value, "seq", pairs)


def per_device(
    fsdp, inputs, lengths, w_query, b_query, w_key, w_value, b_value, w_out, b_out,
    gain_one, shift_one, w_inner, b_inner, w_outer, b_outer, gain_two, shift_two, cotangent,
):
    pages_all, blk, d = inputs.shape
    pages = pages_all // 2
    s = lax.axis_index("seq")
    x_at = lax.div(s, 2)
    direct = fsdp == 8
    ws = (w_query, w_key, w_value, w_out, w_inner, w_outer)
    shards = [w.shape for w in ws]
    width = b_query.shape[0]
    names = (b_query, b_value, b_out, gain_one, shift_one, b_outer, gain_two, shift_two)
    vec = jnp.concatenate(names + (b_inner,)).reshape(12, width)

    def pages_of(array, side):
        return lax.dynamic_slice_in_dim(array, side * pages, pages, 0)

    if direct:
        padded = jnp.pad(vec, ((0, 4), (0, 128 - width)))
        full, xs, cots, gvec = gather_all(inputs, cotangent, ws, padded)
        gvec = gvec[:, :12, :width]
        xa, xb, xc, xd = xs
        ca, cb = cots
    else:
        full = [lax.all_gather(w, "fsdp", axis=0, tiled=True) for w in ws]
        gvec = lax.all_gather(vec, "fsdp", axis=0)
        xa, ca = pages_of(inputs, x_at), pages_of(cotangent, x_at)
        xb = swap(pages_of(inputs, 1 - x_at), SWAP_X)
        cb = swap(pages_of(cotangent, 1 - x_at), SWAP_X)
        xc, xd = swap(xa, SWAP_C), swap(xb, SWAP_C)
    wq, wk, wv, wo, wi, w2 = full
    vec_full = jnp.swapaxes(gvec[:, :8], 0, 1).reshape(8, d).astype(F32)
    bin_full = gvec[:, 8:].reshape(1, -1).astype(F32)

    order = jnp.stack([s, s ^ 2, s ^ 1, s ^ 3]).astype(jnp.int32)
    thr = pages_of(lengths, x_at).astype(jnp.int32)[:, None] - order[None, :] * blk

    q, k, v, p, ctx = attn_fwd(thr, (xa, xb, xc, xd), wq, wk, wv, vec_full)
    out_a, out_b, gm1, dctx, dwo, dwi, dw2, gv_ffn, gbin = ffn(
        ctx, xa, xb, ca, cb, wo, wi, w2, vec_full, bin_full
    )
    dq, dk, dk_send, dv, dv_send = attn_bwd(q, k, v, p, ctx, dctx)
    dkr, dvr = swap(dk_send, SWAP_C), swap(dv_send, SWAP_C)
    gx_a, gx_b, dwq, dwk, dwv, gv_proj = proj(xa, xb, dq, dk, dkr, dv, dvr, gm1, wq, wk, wv)

    gv = jnp.concatenate([gv_proj[:2], gv_ffn[2:]], axis=0)
    grads = (dwq, dwk, dwv, dwo, dwi, dw2)
    by_owner = jnp.concatenate(
        [jnp.swapaxes(gv.reshape(8, fsdp, width), 0, 1), gbin.reshape(fsdp, 4, width)], axis=1
    )
    if direct:
        padded = jnp.pad(by_owner, ((0, 0), (0, 4), (0, 128 - width)))
        tot, output, grad_inputs, tvec = scatter_all(grads, out_a, out_b, gx_a, gx_b, padded, shards)
        tvec = tvec[:12, :width]
    else:
        tot = [
            lax.psum(lax.psum_scatter(g, "fsdp", scatter_dimension=0, tiled=True), "seq").astype(F32)
            for g in grads
        ]
        tvec = lax.psum(lax.psum_scatter(by_owner, "fsdp", scatter_dimension=0, tiled=True)[0], "seq")

        def joined(mine, other):
            here = lax.dynamic_update_slice_in_dim(
                jnp.zeros((pages_all, blk, d), mine.dtype), mine, x_at * pages, 0
            )
            return lax.dynamic_update_slice_in_dim(here, other, (1 - x_at) * pages, 0)

        output = joined(out_a, swap(out_b, SWAP_X))
        grad_inputs = joined(gx_a, swap(gx_b, SWAP_X).astype(F32))
    small = [tvec[i] for i in range(8)]
    g_bq, g_bv, g_bo, g_g1, g_s1, g_bo2, g_g2, g_s2 = small
    g_bi = tvec[8:].reshape(-1)
    t_q, t_k, t_v, t_o, t_i, t_2 = tot
    return (
        output, grad_inputs, t_q, g_bq, t_k, t_v, g_bv, t_o, g_bo, g_g1, g_s1,
        t_i, g_bi, t_2, g_bo2, g_g2, g_s2,
    )


def solution(mesh):
    vec, mat, act = P("fsdp"), P("fsdp", None), P("fsdp", "seq", None)
    return jax.shard_map(
        functools.partial(per_device, mesh.shape["fsdp"]),
        mesh=mesh,
        in_specs=(act, vec, mat, vec, mat, mat, vec, mat, vec, vec, vec, mat, vec, mat, vec, vec, vec, act),
        out_specs=(act, act, mat, vec, mat, mat, vec, mat, vec, vec, vec, mat, vec, mat, vec, vec, vec),
        check_vma=False,
    )
```

time: 1470 us -> 399 us (0.27)
  waiting for transfers between devices: 878 us -> 3 us
  Pallas kernels: 0 us -> 367 us
  matrix products: 255 us -> 0 us
  local copies, waits for them, and re-layouts: 139 us -> 23.1 us
  blocking collectives: 107 us -> 0 us
  other arithmetic: 58.4 us -> 3.51 us
  between operations: 16.8 us -> 0.76 us
    pallas_call x0 -> x6, Pallas kernels: none -> 367 us  [the longest x1 126 us: gather_all(): call(gather_body, (0, sum((16 * w.size for w in ws)), 0), in_specs=[ANY]...]
    reduce_scatter x3 -> x0, waiting for transfers between devices: 358 us -> none  [the longest x1 164 us: per_device(): lax.psum_scatter(grad_w_inner, 'fsdp', scatter_dimension=0, tiled=True)]
    all_gather x8 -> x0, waiting for transfers between devices: 258 us -> none  [the longest x1 80.2 us: per_device(): lax.all_gather(w_outer, 'fsdp', axis=0, tiled=True)]
    dot_general x74 -> x0, matrix products: 255 us -> none  [the longest x8 76.7 us: matmul(): return jnp.dot(left_side, right_side, preferred_element_type=jnp.float32)]
    unnamed x22 -> x0, waiting for transfers between devices: 218 us -> none
    unnamed x2 -> x0, blocking collectives: 75.3 us -> none
    unnamed x135 -> x32, local copies, waits for them, and re-layouts: 80.6 us -> 10.5 us
    psum x1 -> x0, waiting for transfers between devices: 44.3 us -> none  [per_device(): lax.psum(part_w_query.astype(jnp.bfloat16), 'seq').astype(jnp.float32)]
  transfers between devices with their start and end apart: 17 -> 2, of which waited for: 15 -> 2; matrix products, arithmetic and copies ran while one was open for 13% -> 0% of each run, Pallas kernels for 0% -> 0%
where the time goes in v1:
time: 399 us; the launch traced here: 398 us
  Pallas kernels  367 us (92%)
  local copies, waits for them, and re-layouts  23.1 us (6%)
    pallas_call x1, Pallas kernels, gather_all(): call(gather_body, (0, sum((16 * w.size for w in ws)), 0), in_specs=[ANY]...  126 us
    pallas_call x1, Pallas kernels, scatter_all(): call(scatter_body, (0, sum((16 * g.size for g in grads)), 0), in_specs=[A...  116 us
    pallas_call x1, Pallas kernels, ffn(): call(ffn_body, (n * d * (12 * ff + 6 * d), 4 * d * ff * 2 + 12 * n * d *...  60.2 us
    pallas_call x1, Pallas kernels, attn_fwd(): call(attn_fwd_body, (pages * (2 * d * d * (own + 2 * rows) + 4 * own * ro...  32.2 us
    pallas_call x1, Pallas kernels, attn_bwd(): call(attn_bwd_body, (pages * 10 * own * rows * d, pages * (own * rows * H...  19.7 us
    pallas_call x1, Pallas kernels, proj(): call(proj_body, (12 * n * d * d, 12 * d * d + 16 * n * d, 0), grid=(pages...  13.1 us
    unnamed x32, local copies, waits for them, and re-layouts  10.5 us
  transfers between devices with their start and end apart: 2, of which 2 were waited for; matrix products, arithmetic and copies ran while one was open for 0% of the time, Pallas kernels for 0%

profile of v1, /device:TPU:0, one launch (start us, length us, event | category | flops | bytes accessed | tf_op | source)
XLA Modules:
  0.0 397.9 jit_solution(16271143253544336461)
XLA Ops:
  0.7 6.1 %concatenate.13 = bf16[1152]{0:T(1024)(128)(2,1)S(1)} concatenate(bf16[96]{0:T(256)(128)(2,1)} %param.21, bf16[96]{0:T(256)(128)(2,1)} %param.24, bf16[96]{0:T(256)(128)(2,1)} %param.26, bf16[96]{0:T(256)(128)(2,1)} %param.27, bf16[96]{0:T(256)(128)(2,1)} %param.28, bf16[96]{0:T(256)(128)(2,1)} %param.32, bf16[96]{0:T(256)(128)(2,1)} %param.33, bf16[96]{0:T(256)(128)(2,1)} %param.34, ...), dimensions={0} | concatenate | bytes 4608 | tf_op jit(solution)/shard_map/concatenate | solution.py:766
  6.8 0.1 reshape.135
  6.9 0.6 pad.8.vec
  7.5 0.0 copy-start.11
  7.5 126.1 %gather_all.1 = (bf16[4,2,96,768]{3,2,1,0:T(8,128)(2,1)}, bf16[4,2,96,768]{3,2,1,0:T(8,128)(2,1)}, bf16[4,2,96,768]{3,2,1,0:T(8,128)(2,1)}, bf16[4,2,96,768]{3,2...) custom-call(bf16[6,128,768]{2,1,0:T(8,128)(2,1)} %x_in.1, ...), custom_call_target="tpu_custom_call" | custom-call | bytes 14155776 | tf_op jit(solution)/shard_map/gather_all/pallas_call | solution.py:544
  133.6 0.7 convert_bitcast_fusion
  134.3 0.7 slice_convert_fusion
  135.0 0.7 reshape.151.vec
  135.7 0.7 reshape.152.b_in
  136.4 0.0 copy-done.11
  136.4 0.1 dynamic_slice.3
  136.5 0.1 add_multiply_fusion
  136.5 0.7 broadcast_subtract_fusion.thr
  137.2 32.2 %attn_fwd.1 = (bf16[3,256,768]{2,1,0:T(8,128)(2,1)}, bf16[3,512,768]{2,1,0:T(8,128)(2,1)}, bf16[3,512,768]{2,1,0:T(8,128)(2,1)}, bf16[3,12,512,256]{3,2,1,0:T(8,128)(2,1)}, bf16[3,256,768]{2,1,0:T(8,128)(2,1)}) custom-call(s32[3,4]{1,0:T(4,128)} %broadcast_subtract_fusion.thr, bf16[3,128,768]{2,1,0:T(8,128)(2,1)} %get-tuple-element.64.xa, ...), custom_call_target="tpu_custom_call" | custom-call | flops 5737807872 | bytes 22413312 | tf_op jit(solution)/shard_map/attn_fwd/pallas_call | solution.py:90
  169.4 60.2 %ffn.1 = (bf16[3,128,768]{2,1,0:T(8,128)(2,1)}, bf16[3,128,768]{2,1,0:T(8,128)(2,1)}, f32[3,256,768]{2,1,0:T(8,128)}, bf16[3,256,768]{2,1,0:T(8,128)(2,1)}, bf16...) custom-call(bf16[3,256,768]{2,1,0:T(8,128)(2,1)} %get-tuple-element., ...), custom_call_target="tpu_custom_call" | custom-call | flops 24461180928 | bytes 33030144 | tf_op jit(solution)/shard_map/ffn/pallas_call | solution.py:298
  229.6 0.0 copy-start.8
  229.7 0.0 copy-start.7
  229.7 19.7 %attn_bwd.1 = (bf16[3,256,768]{2,1,0:T(8,128)(2,1)}, bf16[3,256,768]{2,1,0:T(8,128)(2,1)}, bf16[3,256,768]{2,1,0:T(8,128)(2,1)}, bf16[3,256,768]{2,1,0:T(8,128)(2,1)}, bf16[3,256,768]{2,1,0:T(8,128)(2,1)}) custom-call(bf16[3,256,768]{2,1,0:T(8,128)(2,1)} %get-tuple-element.72.q, bf16[3,512,768]{2,1,0:T(8,128)(2,1)} %get-tuple-element.73.k, ...), custom_call_target="tpu_custom_call" | custom-call | flops 3019898880 | bytes 21233664 | tf_op jit(solution)/shard_map/attn_bwd/pallas_call | solution.py:169
  249.4 0.5 collective-permute-start
  249.9 0.1 collective-permute-start.1
  249.9 0.5 broadcast.29
  250.5 0.0 copy-done.8
  250.5 0.7 reduce.3
  251.1 0.1 reshape.149
  251.2 0.0 copy-done.7
  251.2 1.3 collective-permute-done.dkr
  252.6 0.0 copy-start.9
  252.6 1.7 collective-permute-done.1.dvr
  254.2 0.0 copy-start.10
  254.2 0.0 copy-done.9
  254.2 1.0 copy-done.10
  255.3 13.1 %proj_bwd.1 = (f32[3,128,768]{2,1,0:T(8,128)}, bf16[3,128,768]{2,1,0:T(8,128)(2,1)}, bf16[768,768]{1,0:T(8,128)(2,1)}, bf16[768,768]{1,0:T(8,128)(2,1)}, bf16[768,768]{1,0:T(8,128)(2,1)}, /*index=5*/f32[8,768]{1,0:T(8,128)}) custom-call(bf16[3,128,768]{2,1,0:T(8,128)(2,1)} %get-tuple-element.64.xa, bf16[3,128,768]{2,1,0:T(8,128)(2,1)} %get-tuple-element.65.xb, ...), custom_call_target="tpu_custom_call" | custom-call | flops 5435817984 | bytes 16515072 | tf_op jit(solution)/shard_map/proj_bwd/pallas_call | solution.py:372
  268.3 0.7 slice.54
  269.1 0.1 reshape.148
  269.2 0.6 select_maximum_fusion.gvec
  269.8 115.7 %scatter_all.1 = (f32[96,768]{1,0:T(8,128)}, f32[96,768]{1,0:T(8,128)}, f32[96,768]{1,0:T(8,128)}, f32[96,768]{1,0:T(8,128)}, f32[96,3072]{1,0:T(8,128)}, /*inde...) custom-call(bf16[4,2,96,768]{3,2,1,0:T(8,128)(2,1)} %bitcast.40, ...), custom_call_target="tpu_custom_call" | custom-call | bytes 113246208 | tf_op jit(solution)/shard_map/scatter_all/pallas_call | solution.py:712
  385.5 1.5 slice_bitcast_fusion
  387.1 0.7 slice.61
  387.7 0.7 reshape.150
  388.4 0.0 copy-start
  388.4 2.5 copy.48
  390.9 0.0 copy-done
  390.9 0.0 copy-start.6
  390.9 0.0 copy-start.5
  390.9 0.0 copy-start.4
  390.9 1.4 copy.49
  392.3 0.0 copy-done.6
  392.3 0.0 copy-start.3
  392.3 0.0 copy-start.2
  392.3 0.7 copy.50
  393.1 0.0 copy-done.5
  393.1 0.7 copy.51
  393.8 0.0 copy-done.4
  393.8 0.7 copy.52
  394.5 0.0 copy-done.3
  394.5 0.7 copy.53
  395.2 0.0 copy-done.2
  395.2 0.0 copy-start.1
  395.2 1.0 copy.54
  396.2 0.7 copy-done.1
  396.9 1.0 copy.55
  (4 shorter events, 0.0 us)
Async XLA Ops:
  7.5 128.9 %copy-start.11 = (s32[6]{0:T(128)S(1)}, s32[6]{0:T(128)}, u32[]{:S(2)}) copy-start(s32[6]{0:T(128)} %param.19) | copy-start | bytes 76
  229.6 20.8 %copy-start.8 = (f32[1,3072]{1,0:T(1,128)S(1)}, f32[1,3072]{1,0:T(1,128)}, u32[]{:S(2)}) copy-start(f32[1,3072]{1,0:T(1,128)} %get-tuple-element.101) | copy-start | bytes 36868
  229.7 21.6 %copy-start.7 = (f32[8,768]{1,0:T(8,128)S(1)}, f32[8,768]{1,0:T(8,128)}, u32[]{:S(2)}) copy-start(f32[8,768]{1,0:T(8,128)} %get-tuple-element.100) | copy-start | bytes 73732
  249.4 3.2 collective-permute-start
  249.9 4.4 %collective-permute-start.1 = (bf16[3,256,768]{2,1,0:T(8,128)(2,1)}, bf16[3,256,768]{2,1,0:T(8,128)(2,1)S(1)}, u32[]{:S(2)}, u32[]{:S(2)}) collective-permute-start(bf16[3,256,768]{2,1,0:T(8,128)(2,1)} %get-tuple-element.87), channel_id=1, source_target_pairs={{0,1},{1,0},{2,3},{3,2},{4,5},{5,4},{6,7},{7,6},{8,9},{9,8},{10,11... | collective-permute-start | bytes 3538952 | tf_op jit(solution)/shard_map/ppermute | solution.py:750
  252.6 1.7 copy-start.9
  254.2 1.0 copy-start.10
  388.4 2.5 copy-start
  390.9 1.4 copy-start.6
  390.9 2.1 copy-start.5
  390.9 2.9 copy-start.4
  392.3 2.2 copy-start.3
  392.3 2.9 copy-start.2
  395.2 1.7 copy-start.1

commit v2 on v1

v2 whole, which is shorter than its diff:
```python
import functools
import math

import jax
import jax.numpy as jnp
from jax import lax
from jax.experimental import pallas as pl
from jax.experimental.pallas import tpu as pltpu
from jax.sharding import PartitionSpec as P

HEADS = 12
HEAD_DIM = 64
PAIR = 2 * HEAD_DIM
NEG = -1e30
EPS = 1e-12
BF = jnp.bfloat16
F32 = jnp.float32
MESH = pl.DeviceIdType.MESH
ANY = pl.BlockSpec(memory_space=pl.ANY)
VM = pl.BlockSpec(memory_space=pltpu.VMEM)
CHUNK = 1024
ROW = 96
VMEM_CAP = 60 << 20

NN = (((1,), (0,)), ((), ()))
NT = (((1,), (1,)), ((), ()))
TN = (((0,), (0,)), ((), ()))


def dot(a, b, dims=NN):
    return lax.dot_general(a, b, dims, preferred_element_type=F32)


def call(body, cost, **kw):
    flops, byts, trans = cost
    params = dict(vmem_limit_bytes=VMEM_CAP)
    params.update(kw.pop("params", {}))
    return pl.pallas_call(
        body,
        compiler_params=pltpu.CompilerParams(**params),
        cost_estimate=pl.CostEstimate(
            flops=int(flops), bytes_accessed=int(byts), transcendentals=int(trans)
        ),
        **kw,
    )


def attn_fwd_body(thr, xall, wq, wk, wv, vec, q_o, k_o, v_o, p_o, c_o, bias):
    page = pl.program_id(0)
    x_all = xall[0]
    own = x_all.shape[0] // 2
    query = (dot(x_all[:own], wq[...]) + vec[0:1, :]).astype(BF)
    q_o[0] = query
    k_o[0] = dot(x_all, wk[...]).astype(BF)
    v_o[0] = (dot(x_all, wv[...]) + vec[1:2, :]).astype(BF)
    blk = x_all.shape[0] // 4
    place = lax.broadcasted_iota(jnp.int32, (blk, own), 0)
    for b in range(4):
        bias[b * blk : (b + 1) * blk, :] = jnp.where(place < thr[page, b], 0.0, NEG)
    low_lane = lax.broadcasted_iota(jnp.int32, (own, PAIR), 1) < HEAD_DIM

    def pair(i, carry):
        cols = pl.ds(pl.multiple_of(i * PAIR, PAIR), PAIR)
        qp = q_o[0, :, cols] * jnp.array(1.0 / math.sqrt(HEAD_DIM), BF)
        kp = k_o[0, :, cols]
        vt = v_o[0, :, cols].T
        outs = []
        for h in range(2):
            keep = low_lane if h == 0 else jnp.logical_not(low_lane)
            qh = jnp.where(keep, qp, jnp.zeros_like(qp))
            st = dot(kp, qh, NT) + bias[...]
            top = jnp.max(st, axis=0, keepdims=True)
            ex = jnp.exp(st - top)
            tot = jnp.sum(ex, axis=0, keepdims=True)
            pt = (ex * (1.0 / tot)).astype(BF)
            p_o[0, 2 * i + h] = pt
            outs.append(dot(vt[h * HEAD_DIM : (h + 1) * HEAD_DIM], pt))
        c_o[0, :, cols] = jnp.concatenate(outs, axis=0).T.astype(BF)
        return carry

    lax.fori_loop(0, HEADS // 2, pair, 0)


def attn_fwd(thr, xall, wq, wk, wv, vec):
    pages, rows, d = xall.shape
    own = rows // 2
    const = lambda p, t: (0, 0)
    by_page = lambda p, t: (p, 0, 0)
    one = pl.Buffered(1)
    return call(
        attn_fwd_body,
        (
            pages * (2 * d * d * (own + 2 * rows) + 4 * own * rows * d),
            pages * rows * d * 2 * 4 + 6 * d * d + pages * HEADS * own * rows * 2,
            pages * HEADS * own * rows,
        ),
        grid_spec=pltpu.PrefetchScalarGridSpec(
            num_scalar_prefetch=1,
            grid=(pages,),
            in_specs=[pl.BlockSpec((1, rows, d), by_page)]
            + [pl.BlockSpec((d, d), const, pipeline_mode=one)] * 3
            + [pl.BlockSpec((8, d), const)],
            out_specs=[
                pl.BlockSpec((1, own, d), by_page),
                pl.BlockSpec((1, rows, d), by_page),
                pl.BlockSpec((1, rows, d), by_page),
                pl.BlockSpec((1, HEADS, rows, own), lambda p, t: (p, 0, 0, 0)),
                pl.BlockSpec((1, own, d), by_page),
            ],
            scratch_shapes=[pltpu.VMEM((rows, own), F32)],
        ),
        out_shape=[
            jax.ShapeDtypeStruct((pages, own, d), BF),
            jax.ShapeDtypeStruct((pages, rows, d), BF),
            jax.ShapeDtypeStruct((pages, rows, d), BF),
            jax.ShapeDtypeStruct((pages, HEADS, rows, own), BF),
            jax.ShapeDtypeStruct((pages, own, d), BF),
        ],
        name="attn_fwd",
    )(thr, xall, wq, wk, wv, vec)


def attn_bwd_body(q, k, v, p, ctx, dctx, dq_o, dk_own, dk_oth, dv_own, dv_oth):
    own = q.shape[1]
    low_lane = lax.broadcasted_iota(jnp.int32, (own, PAIR), 1) < HEAD_DIM
    scale = 1.0 / math.sqrt(HEAD_DIM)

    def pair(i, carry):
        cols = pl.ds(pl.multiple_of(i * PAIR, PAIR), PAIR)
        qp = q[0, :, cols] * jnp.array(scale, BF)
        kp = k[0, :, cols]
        kt = kp.T
        vp = v[0, :, cols]
        dc = dctx[0, :, cols]
        prod = (dc.astype(F32) * ctx[0, :, cols].astype(F32)).T
        dk = None
        dv = None
        dqs = []
        for h in range(2):
            keep = low_lane if h == 0 else jnp.logical_not(low_lane)
            feats = slice(h * HEAD_DIM, (h + 1) * HEAD_DIM)
            dch = jnp.where(keep, dc, jnp.zeros_like(dc))
            qh = jnp.where(keep, qp, jnp.zeros_like(qp))
            pt = p[0, 2 * i + h]
            delta = jnp.sum(prod[feats], axis=0, keepdims=True)
            dpt = dot(vp, dch, NT)
            dst = (pt.astype(F32) * (dpt - delta)).astype(BF)
            dvh = dot(pt, dch)
            dkh = dot(dst, qh)
            dk = dkh if dk is None else dk + dkh
            dv = dvh if dv is None else dv + dvh
            dqs.append(dot(kt[feats], dst))
        dq_o[0, :, cols] = (jnp.concatenate(dqs, axis=0) * scale).T.astype(BF)
        dk_own[0, :, cols] = dk[:own].astype(BF)
        dk_oth[0, :, cols] = dk[own:].astype(BF)
        dv_own[0, :, cols] = dv[:own].astype(BF)
        dv_oth[0, :, cols] = dv[own:].astype(BF)
        return carry

    lax.fori_loop(0, HEADS // 2, pair, 0)


def attn_bwd(q, k, v, p, ctx, dctx):
    pages, own, d = q.shape
    rows = k.shape[1]
    by_page = lambda i: (i, 0, 0)
    o = pl.BlockSpec((1, own, d), by_page)
    r = pl.BlockSpec((1, rows, d), by_page)
    return call(
        attn_bwd_body,
        (pages * 10 * own * rows * d, pages * (own * rows * HEADS * 2 + 10 * own * d * 2), 0),
        grid=(pages,),
        in_specs=[o, r, r, pl.BlockSpec((1, HEADS, rows, own), lambda i: (i, 0, 0, 0)), o, o],
        out_specs=[o] * 5,
        out_shape=[jax.ShapeDtypeStruct((pages, own, d), BF)] * 5,
        name="attn_bwd",
    )(q, k, v, p, ctx, dctx)


def normal_parts(v):
    bell = jnp.exp(v * v * -0.5)
    t = 1.0 / (1.0 + jnp.abs(v) * (0.3275911 / math.sqrt(2.0)))
    tail = t * (
        0.127414796 + t * (-0.142248368 + t * (0.7107068705 + t * (-0.7265760135 + t * 0.5307027145)))
    )
    tail = tail * bell
    return jnp.where(v >= 0.0, 1.0 - tail, tail), bell * (1.0 / math.sqrt(2.0 * math.pi))


def row_norm(v):
    centered = v - jnp.mean(v, -1, keepdims=True)
    inv = lax.rsqrt(jnp.mean(centered * centered, -1, keepdims=True) + EPS)
    return centered * inv, inv


def norm_back(e, n, inv):
    return inv * (e - jnp.mean(e, -1, keepdims=True) - n * jnp.mean(e * n, -1, keepdims=True))


def ffn_body(
    ctx, xall, cown, wo, wi_h, w2_h, vec, b_in,
    out, gm1_o, dctx_o, dwo_o, dwi_h, dw2_h, gvec, gbin,
    wi, w2, act, din, dgel, hid, gout, gatt, n1s, h1s, accs, r1s, dwi, dw2, lsem, osem,
):
    n, ff = act.shape
    pages, own, d = ctx.shape

    def cols_of(j):
        return pl.ds(pl.multiple_of(j * CHUNK, CHUNK), CHUNK)

    def loads(j):
        cols = cols_of(j)
        return (
            pltpu.make_async_copy(wi_h.at[:, cols], wi.at[:, cols], lsem.at[0, j]),
            pltpu.make_async_copy(w2_h.at[cols, :], w2.at[cols, :], lsem.at[1, j]),
        )

    def store_w2(j):
        return pltpu.make_async_copy(dw2.at[cols_of(j), :], dw2_h.at[cols_of(j), :], osem.at[0, j])

    def store_wi(j):
        return pltpu.make_async_copy(dwi.at[:, cols_of(j)], dwi_h.at[:, cols_of(j)], osem.at[1, j])

    n_chunks = ff // CHUNK
    for j in range(n_chunks):
        for copy in loads(j):
            copy.start()
    gvec[...] = jnp.zeros_like(gvec)

    def add(row, value):
        gvec[row : row + 1, :] += jnp.sum(value, 0, keepdims=True)

    for p in range(pages):
        r = slice(p * own, (p + 1) * own)
        mid = xall[p].astype(F32) + (dot(ctx[p], wo[...]) + vec[2:3, :])
        n1, r1 = row_norm(mid)
        n1s[r, :] = n1
        r1s[r, :] = jnp.broadcast_to(r1, (own, 128))
        h1 = n1 * vec[3:4, :] + vec[4:5, :]
        h1s[r, :] = h1
        hid[r, :] = h1.astype(BF)
    accs[...] = jnp.zeros_like(accs)

    def up(j, carry):
        cols = cols_of(j)
        for copy in loads(j):
            copy.wait()
        pre = dot(hid[...], wi[:, cols]) + b_in[:, cols]
        big, bell = normal_parts(pre)
        a = (pre * big).astype(BF)
        dgel[:, cols] = (big + pre * bell).astype(BF)
        act[:, cols] = a
        accs[...] += dot(a, w2[cols, :])
        return carry

    lax.fori_loop(0, n_chunks, up, 0)
    for p in range(pages):
        r = slice(p * own, (p + 1) * own)
        mid = h1s[r, :] + (accs[r, :] + vec[5:6, :])
        n2, r2 = row_norm(mid)
        out[p] = (n2 * vec[6:7, :] + vec[7:8, :]).astype(BF)
        cot = cown[p].astype(F32)
        gm2 = norm_back(cot * vec[6:7, :], n2, r2)
        go = gm2.astype(BF)
        gout[r, :] = go
        accs[r, :] = gm2
        add(5, go.astype(F32))
        add(6, cot * n2)
        add(7, cot)

    def down(j, carry):
        cols = cols_of(j)
        di = (dot(gout[...], w2[cols, :], NT) * dgel[:, cols].astype(F32)).astype(BF)
        din[:, cols] = di
        accs[...] += dot(di, wi[:, cols], NT)
        gbin[:, cols] = jnp.sum(di.astype(F32), 0, keepdims=True)
        dw2[cols, :] = dot(act[:, cols], gout[...], TN).astype(BF)
        store_w2(j).start()
        return carry

    lax.fori_loop(0, n_chunks, down, 0)
    for p in range(pages):
        r = slice(p * own, (p + 1) * own)
        gh = accs[r, :]
        n1 = n1s[r, :]
        gm1 = norm_back(gh * vec[3:4, :], n1, r1s[r, 0:1])
        gm1_o[p] = gm1
        ga = gm1.astype(BF)
        gatt[r, :] = ga
        dctx_o[p] = dot(ga, wo[...], NT).astype(BF)
        add(2, ga.astype(F32))
        add(3, gh * n1)
        add(4, gh)
    hid_t = hid[...].T

    def grads(j, carry):
        cols = cols_of(j)
        dwi[:, cols] = dot(hid_t, din[:, cols]).astype(BF)
        store_wi(j).start()
        return carry

    lax.fori_loop(0, n_chunks, grads, 0)
    dwo_o[...] = dot(ctx[...].reshape(n, d), gatt[...], TN).astype(BF)
    for j in range(n_chunks):
        store_w2(j).wait()
        store_wi(j).wait()


def ffn(ctx, xall, cown, wo, wi, w2, vec, b_in):
    pages, own, d = ctx.shape
    ff = wi.shape[1]
    n = pages * own
    sds = jax.ShapeDtypeStruct
    vm = pltpu.VMEM
    dma = pltpu.SemaphoreType.DMA
    return call(
        ffn_body,
        (n * d * (12 * ff + 6 * d), 4 * d * ff * 2 + 12 * n * d * 2, n * ff),
        grid=(1,),
        in_specs=[
            pl.BlockSpec((pages, own, d), lambda i: (0, 0, 0)),
            pl.BlockSpec((pages, own, d), lambda i: (0, 0, 0)),
            VM, VM, ANY, ANY, VM, VM,
        ],
        out_specs=[VM] * 4 + [ANY, ANY, VM, VM],
        out_shape=[
            sds((pages, own, d), BF), sds((pages, own, d), F32), sds((pages, own, d), BF),
            sds((d, d), BF), sds((d, ff), BF), sds((ff, d), BF), sds((8, d), F32), sds((1, ff), F32),
        ],
        scratch_shapes=[
            vm((d, ff), BF), vm((ff, d), BF), vm((n, ff), BF), vm((n, ff), BF), vm((n, ff), BF),
            vm((n, d), BF), vm((n, d), BF), vm((n, d), BF), vm((n, d), F32), vm((n, d), F32),
            vm((n, d), F32), vm((n, 128), F32), vm((d, ff), BF), vm((ff, d), BF),
            dma((2, ff // CHUNK)), dma((2, ff // CHUNK)),
        ],
        params=dict(vmem_limit_bytes=63 << 20),
        name="ffn",
    )(ctx, xall, cown, wo, wi, w2, vec, b_in)


def proj_body(
    xall, dq, dk, dkr, dv, dvr, gm1, wq, wk, wv,
    ga_o, gb_o, dwq_o, dwk_o, dwv_o, gvec, x_all, dq_all, dk_all, dv_all,
):
    page = pl.program_id(0)
    own = xall.shape[1]
    blk = own // 2
    here = pl.ds(pl.multiple_of(page * own, own), own)
    x_all[here, :] = xall[0]
    dq_v = dq[0]
    dk_v = (dk[0].astype(F32) + dkr[0].astype(F32)).astype(BF)
    dv_v = (dv[0].astype(F32) + dvr[0].astype(F32)).astype(BF)
    dq_all[here, :] = dq_v
    dk_all[here, :] = dk_v
    dv_all[here, :] = dv_v
    gx = gm1[0] + dot(dq_v, wq[...], NT) + dot(dk_v, wk[...], NT) + dot(dv_v, wv[...], NT)
    ga_o[0] = gx[:blk]
    gb_o[0] = gx[blk:].astype(BF)

    @pl.when(page == 0)
    def _():
        gvec[...] = jnp.zeros_like(gvec)

    gvec[0:1, :] += jnp.sum(dq_v.astype(F32), 0, keepdims=True)
    gvec[1:2, :] += jnp.sum(dv_v.astype(F32), 0, keepdims=True)

    @pl.when(page == pl.num_programs(0) - 1)
    def _():
        x_t = x_all[...].T
        dwq_o[...] = dot(x_t, dq_all[...]).astype(BF)
        dwk_o[...] = dot(x_t, dk_all[...]).astype(BF)
        dwv_o[...] = dot(x_t, dv_all[...]).astype(BF)


def proj(xall, dq, dk, dkr, dv, dvr, gm1, wq, wk, wv):
    pages, own, d = dq.shape
    blk = own // 2
    n = pages * own
    by_page = lambda p: (p, 0, 0)
    const = lambda p: (0, 0)
    one = pl.Buffered(1)
    half = pl.BlockSpec((1, blk, d), by_page)
    whole = pl.BlockSpec((1, own, d), by_page)
    square = pl.BlockSpec((d, d), const, pipeline_mode=one)
    return call(
        proj_body,
        (12 * n * d * d, 12 * d * d + 16 * n * d, 0),
        grid=(pages,),
        in_specs=[whole] * 7 + [square] * 3,
        out_specs=[half, half] + [square] * 3 + [pl.BlockSpec((8, d), const)],
        out_shape=[
            jax.ShapeDtypeStruct((pages, blk, d), F32),
            jax.ShapeDtypeStruct((pages, blk, d), BF),
        ]
        + [jax.ShapeDtypeStruct((d, d), BF)] * 3
        + [jax.ShapeDtypeStruct((8, d), F32)],
        scratch_shapes=[pltpu.VMEM((n, d), BF)] * 4,
        name="proj_bwd",
    )(xall, dq, dk, dkr, dv, dvr, gm1, wq, wk, wv)


def place():
    f, s = lax.axis_index("fsdp"), lax.axis_index("seq")
    return lax.div(f, 2), lax.rem(f, 2), lax.div(s, 2), lax.rem(s, 2)


def at(z, y, x, c):
    return {"fsdp": 2 * z + y, "seq": 2 * x + c}


def meet(others):
    barrier = pltpu.get_barrier_semaphore()
    for other in others:
        pl.semaphore_signal(barrier, inc=1, device_id=other, device_id_type=MESH)
    pl.semaphore_wait(barrier, len(others))


def remote(src, dst, send, recv, other):
    return pltpu.make_async_remote_copy(
        src_ref=src, dst_ref=dst, send_sem=send, recv_sem=recv,
        device_id=other, device_id_type=MESH,
    )


def begin(copy):
    copy.start()
    return copy


class Spread:
    def __init__(self, where, src, dst, row0, col0, width, sems, key):
        self.z, self.y, self.x, self.c = where
        z, y, x, c = where
        zs, zr, fs, ys, yr, xs, xr, cs, cr, lo = sems
        k = key
        cols = pl.ds(pl.multiple_of(col0 + width * c, 128), width)
        full = pl.ds(row0, ROW)
        mine = pl.ds(pl.multiple_of(row0 + (ROW // 2) * x, 16), ROW // 2)
        near, far, across = z + 1 - 2 * lax.rem(z, 2), lax.rem(z + 2, 4), 3 - z
        self.inner = jnp.logical_or(z == 1, z == 2)
        self.local = lambda: pltpu.make_async_copy(src.at[full, cols], dst.at[z, y, full, cols], lo.at[k])

        def send(block, n, target, sem):
            from_ref = src.at[full, cols] if block is None else dst.at[block, y, full, cols]
            b = z if block is None else block
            return remote(from_ref, dst.at[b, y, full, cols], sem, zr.at[k + (n,)], at(target, y, x, c))

        self.a = lambda: send(None, 0, near, zs.at[k + (0,)])
        self.b = lambda: send(None, 1, far, zs.at[k + (1,)])
        self.d = lambda: send(None, 2, across, zs.at[k + (2,)])
        self.fwd = lambda: send(far, 2, near, fs.at[k])
        yv = lambda: dst.at[:, y, mine, cols]
        self.ycopy = lambda: remote(yv(), yv(), ys.at[k], yr.at[k], at(z, 1 - y, x, c))
        xv = lambda: dst.at[:, 1 - y, mine, cols]
        self.xcopy = lambda: remote(xv(), xv(), xs.at[k], xr.at[k], at(z, y, 1 - x, c))
        cv = lambda: dst.at[:, :, full, cols]
        self.ccopy = lambda: remote(cv(), cv(), cs.at[k], cr.at[k], at(z, y, x, 1 - c))

    def along_z(self):
        self.local().start()
        self.b().start()
        self.a().start()

        @pl.when(self.inner)
        def _():
            self.d().start()

    def forward(self):
        self.b().wait_recv()

        @pl.when(self.inner)
        def _():
            self.fwd().start()

    def along_y(self):
        self.a().wait_recv()
        self.d().wait_recv()
        self.local().wait()
        self.ycopy().start()

    def along_x(self):
        self.ycopy().wait_recv()
        self.xcopy().start()

    def to_core(self):
        self.xcopy().wait_recv()
        self.ccopy().start()

    def arrive(self):
        self.ccopy().wait_recv()

    def drain(self):
        self.a().wait_send()
        self.b().wait_send()

        @pl.when(self.inner)
        def _():
            self.d().wait_send()
            self.fwd().wait_send()

        self.ycopy().wait_send()
        self.xcopy().wait_send()
        self.ccopy().wait_send()


def spread_sems(*lead):
    dma = pltpu.SemaphoreType.DMA
    return [dma(lead + (3,)), dma(lead + (3,))] + [dma(lead)] * 8


GROUPS = 3
GCOLS = 256
REST = 9


def fwd_body(
    thr, x_in, cot, wq, wk, wv, wo, wi, w2, *refs,
):
    smalls = refs[:9]
    (gq, gk, gv, go, gi, g2, xall, cown, q_o, k_o, v_o, c_o, p_o, vec, b_in) = refs[9:24]
    bias, pbuf, vpk, gvec = refs[24:28]
    qs, rs = refs[28:38], refs[38:48]
    asend, arecv, aloc, vs, vr, ps = refs[48:]
    z, y, x, c = where = place()
    f = 2 * z + y
    pages, rows = xall.shape[0], xall.shape[1]
    own, blk = rows // 2, rows // 4
    width = smalls[0].shape[-1]
    for i in range(8):
        vpk[i : i + 1, :width] = smalls[i][...].astype(F32).reshape(1, width)
    for i in range(3):
        vpk[8 + i : 9 + i, :] = smalls[8][:, 128 * i : 128 * (i + 1)].astype(F32).reshape(1, 128)
    gvec[f] = vpk[...]
    x_peer, c_peer = at(z, y, 1 - x, c), at(z, y, x, 1 - c)
    meet([{"fsdp": lax.rem(f + k + 1, 8)} for k in range(7)] + [x_peer, c_peer])

    groups = [
        [Spread(where, src, dst, 0, GCOLS * g, GCOLS // 2, qs, (g, w)) for w, (src, dst) in enumerate(((wq, gq), (wk, gk), (wv, gv)))]
        for g in range(GROUPS)
    ]

    def each(g, step):
        for part in groups[g]:
            getattr(part, step)()

    mine, sent = pl.ds(pages * x, pages), pl.ds(pages * (1 - x), pages)

    def band(b):
        return xall.at[:, pl.ds(blk * b, blk), :]

    to_b = remote(x_in.at[sent], band(1), asend.at[0], arecv.at[0], x_peer)
    to_c = remote(x_in.at[mine], band(2), asend.at[1], arecv.at[1], c_peer)
    to_d = remote(band(1), band(3), asend.at[2], arecv.at[2], c_peer)
    cot_b = remote(cot.at[sent], cown.at[:, pl.ds(blk, blk), :], asend.at[3], arecv.at[3], x_peer)
    keep_x = pltpu.make_async_copy(x_in.at[mine], band(0), aloc.at[0])
    keep_c = pltpu.make_async_copy(cot.at[mine], cown.at[:, pl.ds(0, blk), :], aloc.at[1])
    vecs = [
        remote(vpk, gvec.at[f], vs.at[k], vr.at[k], {"fsdp": lax.rem(f + k + 1, 8)}) for k in range(7)
    ]
    each(0, "along_z")
    to_b.start()
    keep_x.start()
    to_c.start()
    for copy in vecs:
        copy.start()
    each(1, "along_z")
    place_row = lax.broadcasted_iota(jnp.int32, (blk, own), 0)
    for page in range(pages):
        for b in range(4):
            bias[page, b * blk : (b + 1) * blk, :] = jnp.where(place_row < thr[page, b], 0.0, NEG)
    each(0, "forward")
    each(0, "along_y")
    each(2, "along_z")
    each(1, "forward")
    each(1, "along_y")
    each(0, "along_x")
    each(2, "forward")
    each(2, "along_y")
    to_b.wait_recv()
    to_d.start()
    each(1, "along_x")
    for copy in vecs:
        copy.wait_recv()
    for i in range(8):
        vec[i : i + 1, :] = jnp.concatenate([gvec[j, i : i + 1, :width] for j in range(8)], axis=1)
    for j in range(8):
        for i in range(3):
            b_in[:, (3 * j + i) * 128 : (3 * j + i + 1) * 128] = gvec[j, 8 + i : 9 + i, :]
    each(0, "to_core")
    keep_c.start()
    keep_x.wait()
    to_c.wait_recv()
    to_d.wait_recv()
    each(0, "arrive")

    def rest(p, step):
        def run(src, dst, row0, col0):
            getattr(Spread(where, src, dst, row0, col0, 384, rs, (p,)), step)()

        @pl.when(p == 0)
        def _():
            run(wo, go, 0, 0)

        @pl.when(jnp.logical_and(p >= 1, p < 5))
        def _():
            run(wi, gi, 0, 768 * (p - 1))

        @pl.when(jnp.logical_and(p >= 5, p < REST))
        def _():
            run(w2, g2, ROW * (p - 5), 0)

    low_lane = lax.broadcasted_iota(jnp.int32, (own, PAIR), 1) < HEAD_DIM
    lags = (("forward", 2), ("along_y", 3), ("along_x", 6), ("to_core", 9))

    def tick(t):
        @pl.when(t < REST)
        def _():
            rest(t, "along_z")

        for step, lag in lags:
            rest(t - lag, step)

    def p_copy(page, pair, slot):
        return pltpu.make_async_copy(pbuf.at[slot], p_o.at[page, pl.ds(2 * pair, 2)], ps.at[slot])

    def unit(it, carry):
        g, page = lax.div(it, pages), lax.rem(it, pages)

        @pl.when(it == 0)
        def _():
            each(2, "along_x")
            each(1, "to_core")

        @pl.when(it == 1)
        def _():
            each(2, "to_core")
            cot_b.start()

        @pl.when(it == pages)
        def _():
            each(1, "arrive")

        @pl.when(it == 2 * pages)
        def _():
            each(2, "arrive")

        gcols = pl.ds(pl.multiple_of(g * GCOLS, GCOLS), GCOLS)
        x_all = xall[page]
        d = x_all.shape[1]
        query = (dot(x_all[:own], gq[:, :, :, gcols].reshape(d, GCOLS)) + vec[0:1, gcols]).astype(BF)
        keys = dot(x_all, gk[:, :, :, gcols].reshape(d, GCOLS)).astype(BF)
        vals = (dot(x_all, gv[:, :, :, gcols].reshape(d, GCOLS)) + vec[1:2, gcols]).astype(BF)
        q_o[page, :, gcols] = query
        k_o[page, :, gcols] = keys
        v_o[page, :, gcols] = vals
        for half in range(2):
            lanes = slice(half * PAIR, (half + 1) * PAIR)
            pair = 2 * g + half

            @pl.when(it > 0)
            def _():
                p_copy(page, pair, half).wait()

            qp = query[:, lanes] * jnp.array(1.0 / math.sqrt(HEAD_DIM), BF)
            kp = keys[:, lanes]
            vt = vals[:, lanes].T
            outs = []
            for h in range(2):
                keep = low_lane if h == 0 else jnp.logical_not(low_lane)
                qh = jnp.where(keep, qp, jnp.zeros_like(qp))
                st = dot(kp, qh, NT) + bias[page]
                top = jnp.max(st, axis=0, keepdims=True)
                ex = jnp.exp(st - top)
                tot = jnp.sum(ex, axis=0, keepdims=True)
                pt = (ex * (1.0 / tot)).astype(BF)
                pbuf[half, h] = pt
                outs.append(dot(vt[h * HEAD_DIM : (h + 1) * HEAD_DIM], pt))
            p_copy(page, pair, half).start()
            cols = pl.ds(pl.multiple_of(pair * PAIR, PAIR), PAIR)
            c_o[page, :, cols] = jnp.concatenate(outs, axis=0).T.astype(BF)
            tick(2 * it + half)
        return carry

    lax.fori_loop(0, GROUPS * pages, unit, 0)
    n_ticks = 2 * GROUPS * pages
    lax.fori_loop(n_ticks, REST + lags[-1][1], lambda t, carry: (tick(t), carry)[1], 0)
    for half in range(2):
        p_copy(0, 0, half).wait()

    def finish(p, carry):
        rest(p, "arrive")
        rest(p, "drain")
        return carry

    lax.fori_loop(0, REST, finish, 0)
    for g in range(GROUPS):
        each(g, "drain")
    cot_b.wait_recv()
    for copy in vecs + [to_b, to_c, to_d, cot_b]:
        copy.wait_send()
    keep_c.wait()


def fwd(thr, x_in, cot, ws, smalls):
    pages_all, blk, d = x_in.shape
    pages, own, rows = pages_all // 2, 2 * blk, 4 * blk
    dma = pltpu.SemaphoreType.DMA
    sds = jax.ShapeDtypeStruct
    shapes = [(4, 2) + w.shape for w in ws]
    ff = ws[4].shape[1]
    res = call(
        fwd_body,
        (pages * 2 * d * d * (own + 2 * rows), sum(16 * w.size for w in ws), pages * HEADS * own * rows),
        in_specs=[pl.BlockSpec(memory_space=pltpu.SMEM)] + [ANY] * 8 + [VM] * 9,
        out_specs=[VM] * 3 + [ANY] * 3 + [VM, ANY, VM, VM, VM, VM, ANY, VM, VM],
        out_shape=[sds(s, BF) for s in shapes]
        + [
            sds((pages, rows, d), BF), sds((pages, own, d), BF),
            sds((pages, own, d), BF), sds((pages, rows, d), BF), sds((pages, rows, d), BF),
            sds((pages, own, d), BF), sds((pages, HEADS, rows, own), BF),
            sds((8, d), F32), sds((1, ff), F32),
        ],
        scratch_shapes=[
            pltpu.VMEM((pages, rows, own), F32),
            pltpu.VMEM((2, 2, rows, own), BF),
            pltpu.VMEM((16, 128), F32),
            pltpu.VMEM((8, 16, 128), F32),
        ]
        + spread_sems(GROUPS, 3)
        + spread_sems(REST)
        + [dma((4,)), dma((4,)), dma((2,)), dma((7,)), dma((7,)), dma((2,))],
        params=dict(collective_id=0, has_side_effects=True),
        name="gather_attention",
    )(thr, x_in, cot, *ws, *smalls)
    full = [r.reshape(-1, r.shape[-1]) for r in res[:6]]
    return full, res[6:]


def neighbours(z, y, x, c):
    n_z = 4
    zs = [at(lax.rem(z + k, n_z), y, x, c) for k in range(1, n_z)]
    far = [at(lax.rem(z + k, n_z), 1 - y, x, c) for k in range(n_z)]
    return zs + far + [at(z, y, 1 - x, c), at(z, y, x, 1 - c)]


def piece_views(wq, wk, wv, wo, wi, w2, lead):
    views = []

    def add(ref, row0, col0):
        def view(sel, rows, cols):
            r0, nr = rows
            c0, nc = cols
            r = pl.ds(row0 + r0, nr)
            c = pl.ds(col0 + c0, nc)
            return ref.at[sel + (r, c)] if lead else ref.at[r, c]

        views.append(view)

    for ref in (wq, wk, wv, wo):
        add(ref, 0, 0)
    for j in range(4):
        add(wi, 0, 768 * j)
    for j in range(4):
        add(w2, ROW * j, 0)
    return views


ALL = slice(None)


def rstart(*a):
    return begin(remote(*a))


def scatter_body(
    gq, gk, gv, go, gi, g2, res, gx_a, gx_b, gvec,
    oq, ok, ov, oo, oi, o2, fin_out, gx, ovec,
    acc, rc, rx, ry, rz, fin, rf, rgx, vecin, vtot, vx,
    lsem, cs, cr, xs, xr, ys, yr, zs, zr, fs, fr, es, er, asend, arecv, aloc, vs, vr, us, ur,
):
    z, y, x, c = place()
    f = 2 * z + y
    meet(neighbours(z, y, x, c) + [at(z, y, 1 - x, 1 - c)])
    x_peer, c_peer, y_peer = at(z, y, 1 - x, c), at(z, y, x, 1 - c), at(z, 1 - y, x, c)
    own_pages = pl.ds(3 * x, 3)
    other_pages = pl.ds(3 * (1 - x), 3)
    src = piece_views(gq, gk, gv, go, gi, g2, True)
    dst = piece_views(oq, ok, ov, oo, oi, o2, False)
    n = len(src)
    hr = ROW // 2
    half_cols = (pl.multiple_of(c * 384, 128), 384)
    their_cols = (pl.multiple_of((1 - c) * 384, 128), 384)
    full = (0, ROW)
    mine = pl.ds(pl.multiple_of(x * hr, 16), hr)
    theirs = pl.ds(pl.multiple_of((1 - x) * hr, 16), hr)
    wide = [p % 2 == 0 for p in range(n)]

    back_x = rstart(gx_b, rgx, asend.at[0], arecv.at[0], x_peer)
    vecs = []
    for k in range(7):
        to = lax.rem(f + k + 1, 8)
        vecs.append(rstart(gvec.at[to], vecin.at[k], vs.at[k], vr.at[k], {"fsdp": to}))
    keep_out = pltpu.make_async_copy(res.at[:, pl.ds(0, 128), :], fin_out.at[own_pages], aloc.at[0])
    keep_out.start()
    mine_first = []
    to_core = []
    for p in range(n):
        copy = pltpu.make_async_copy(src[p]((ALL, ALL), full, half_cols), acc.at[p], lsem.at[p])
        copy.start()
        mine_first.append(copy)
        to_core.append(
            rstart(src[p]((ALL, ALL), full, their_cols), rc.at[p], cs.at[p], cr.at[p], c_peer)
        )
    back_out = rstart(res.at[:, pl.ds(128, 128), :], fin_out.at[own_pages], asend.at[1], arecv.at[1], x_peer)

    gx[own_pages] = gx_a[...]
    along_x, along_y, along_z, finals, ends = [], [], [], [], []
    vec_x = []
    for t in range(n + 5):
        p = t
        if p < n:
            mine_first[p].wait()
            to_core[p].wait_recv()
            acc[p] = (acc[p].astype(F32) + rc[p].astype(F32)).astype(BF)
            if wide[p]:
                along_x.append(
                    rstart(acc.at[p, :, 1 - y, theirs, :], rx.at[p, :, 0], xs.at[p], xr.at[p], x_peer)
                )
            else:
                along_x.append(
                    rstart(acc.at[p, :, :, theirs, :], rx.at[p], xs.at[p], xr.at[p], x_peer)
                )
        p = t - 1
        if 0 <= p < n:
            along_x[p].wait_recv()
            if wide[p]:
                acc[p, :, 1 - y, mine, :] = (
                    acc[p, :, 1 - y, mine, :].astype(F32) + rx[p, :, 0].astype(F32)
                ).astype(BF)
            else:
                acc[p, :, :, mine, :] = (
                    acc[p, :, :, mine, :].astype(F32) + rx[p].astype(F32)
                ).astype(BF)
            along_y.append(
                rstart(acc.at[p, :, 1 - y, mine, :], ry.at[p], ys.at[p], yr.at[p], y_peer)
            )
        p = t - 2
        if 0 <= p < n:
            along_y[p].wait_recv()
            acc[p, :, y, mine, :] = (
                acc[p, :, y, mine, :].astype(F32) + ry[p].astype(F32)
            ).astype(BF)
            group = []
            for k in range(3):
                to = lax.rem(z + k + 1, 4)
                if wide[p]:
                    a, b = acc.at[p, to, y], rz.at[p, k]
                else:
                    a, b = acc.at[p, to, y, mine, :], rz.at[p, k, pl.ds(0, hr)]
                group.append(rstart(a, b, zs.at[p, k], zr.at[p, k], at(to, y, x, c)))
            along_z.append(group)
        p = t - 3
        if 0 <= p < n:
            for copy in along_z[p]:
                copy.wait_recv()
            if wide[p]:
                total = acc[p, z, y].astype(F32)
                for k in range(3):
                    total = total + rz[p, k].astype(F32)
                fin[p] = total.astype(BF)
                finals.append(rstart(fin.at[p], rf.at[p], fs.at[p], fr.at[p], x_peer))
            else:
                total = acc[p, z, y, mine, :].astype(F32)
                for k in range(3):
                    total = total + rz[p, k, :hr].astype(F32)
                fin[p, :hr] = total.astype(BF)
                finals.append(
                    rstart(fin.at[p, pl.ds(0, hr)], rf.at[p, pl.ds(0, hr)], fs.at[p], fr.at[p], x_peer)
                )
        p = t - 4
        if 0 <= p < n:
            finals[p].wait_recv()
            if wide[p]:
                dst[p]((), full, half_cols)[...] = fin[p].astype(F32) + rf[p].astype(F32)
            else:
                dst[p]((), (pl.multiple_of(x * hr, 16), hr), half_cols)[...] = fin[p, :hr].astype(F32)
                dst[p]((), (pl.multiple_of((1 - x) * hr, 16), hr), half_cols)[...] = rf[p, :hr].astype(F32)
            view = dst[p]((), full, half_cols)
            ends.append(rstart(view, view, es.at[p], er.at[p], c_peer))
        if t == 1:
            total = gvec[f]
            for copy in vecs:
                copy.wait_recv()
            for k in range(7):
                total = total + vecin[k]
            vtot[...] = total
            vec_x = [
                rstart(vtot, vx.at[0], us.at[0], ur.at[0], x_peer),
            ]
        if t == 3:
            vec_x[0].wait_recv()
            vx[1] = vtot[...] + vx[0]
            vec_x.append(rstart(vx.at[1], vx.at[2], us.at[1], ur.at[1], c_peer))
        if t == 5:
            back_x.wait_recv()
            gx[other_pages] = rgx[...].astype(F32)
    vec_x[1].wait_recv()
    ovec[...] = vx[1] + vx[2]
    for copy in ends:
        copy.wait_recv()
    back_out.wait_recv()
    keep_out.wait()
    for group in along_z:
        for copy in group:
            copy.wait_send()
    for copy in to_core + along_x + along_y + finals + ends + vecs + vec_x + [back_x, back_out]:
        copy.wait_send()


def scatter_all(grads, out, gx_a, gx_b, gvec, shards):
    dma = pltpu.SemaphoreType.DMA
    n = 12
    pages, own, d = out.shape
    blk = own // 2
    views = [g.reshape((4, 2) + shape) for g, shape in zip(grads, shards)]
    vmem = pltpu.VMEM
    res = call(
        scatter_body,
        (0, sum(16 * g.size for g in grads), 0),
        in_specs=[ANY] * 6 + [ANY, VM, ANY, VM],
        out_specs=[VM] * 6 + [ANY, VM, VM],
        out_shape=[jax.ShapeDtypeStruct(shape, F32) for shape in shards]
        + [
            jax.ShapeDtypeStruct((2 * pages, blk, d), BF),
            jax.ShapeDtypeStruct((2 * pages, blk, d), F32),
            jax.ShapeDtypeStruct(gvec.shape[1:], F32),
        ],
        scratch_shapes=[
            vmem((n, 4, 2, ROW, 384), BF),
            vmem((n, 4, 2, ROW, 384), BF),
            vmem((n, 4, 2, ROW // 2, 384), BF),
            vmem((n, 4, ROW // 2, 384), BF),
            vmem((n, 3, ROW, 384), BF),
            vmem((n, ROW, 384), BF),
            vmem((n, ROW, 384), BF),
            vmem((pages, blk, d), BF),
            vmem((7,) + gvec.shape[1:], F32),
            vmem(gvec.shape[1:], F32),
            vmem((3,) + gvec.shape[1:], F32),
            dma((n,)), dma((n,)), dma((n,)), dma((n,)), dma((n,)), dma((n,)), dma((n,)),
            dma((n, 3)), dma((n, 3)), dma((n,)), dma((n,)), dma((n,)), dma((n,)),
            dma((2,)), dma((2,)), dma((1,)), dma((7,)), dma((7,)), dma((2,)), dma((2,)),
        ],
        params=dict(collective_id=1, has_side_effects=True),
        name="scatter_all",
    )(*views, out, gx_a, gx_b, gvec)
    return res[:6], res[6], res[7], res[8]


SWAP_X = [(0, 2), (2, 0), (1, 3), (3, 1)]
SWAP_C = [(0, 1), (1, 0), (2, 3), (3, 2)]


def swap(value, pairs):
    return lax.ppermute(value, "seq", pairs)


def per_device(
    fsdp, inputs, lengths, w_query, b_query, w_key, w_value, b_value, w_out, b_out,
    gain_one, shift_one, w_inner, b_inner, w_outer, b_outer, gain_two, shift_two, cotangent,
):
    pages_all, blk, d = inputs.shape
    pages = pages_all // 2
    s = lax.axis_index("seq")
    x_at = lax.div(s, 2)
    direct = fsdp == 8
    ws = (w_query, w_key, w_value, w_out, w_inner, w_outer)
    shards = [w.shape for w in ws]
    width = b_query.shape[0]
    names = (b_query, b_value, b_out, gain_one, shift_one, b_outer, gain_two, shift_two)

    def pages_of(array, side):
        return lax.dynamic_slice_in_dim(array, side * pages, pages, 0)

    order = jnp.stack([s, s ^ 2, s ^ 1, s ^ 3]).astype(jnp.int32)
    thr = pages_of(lengths, x_at).astype(jnp.int32)[:, None] - order[None, :] * blk
    if direct:
        lanes = tuple(v.reshape(1, -1) for v in names + (b_inner,))
        full, rest = fwd(thr, inputs, cotangent, ws, lanes)
        wq, wk, wv, wo, wi, w2 = full
        xall, cown, q, k, v, ctx, p, vec_full, bin_full = rest
    else:
        wq, wk, wv, wo, wi, w2 = [lax.all_gather(w, "fsdp", axis=0, tiled=True) for w in ws]
        vec = jnp.concatenate(names + (b_inner,)).reshape(12, width)
        gvec = lax.all_gather(vec, "fsdp", axis=0)
        vec_full = jnp.swapaxes(gvec[:, :8], 0, 1).reshape(8, d).astype(F32)
        bin_full = gvec[:, 8:].reshape(1, -1).astype(F32)

        def own_rows(array):
            other = swap(pages_of(array, 1 - x_at), SWAP_X)
            return jnp.concatenate([pages_of(array, x_at), other], axis=1)

        xown, cown = own_rows(inputs), own_rows(cotangent)
        xall = jnp.concatenate([xown, swap(xown, SWAP_C)], axis=1)
        q, k, v, p, ctx = attn_fwd(thr, xall, wq, wk, wv, vec_full)
    out, gm1, dctx, dwo, dwi, dw2, gv_ffn, gbin = ffn(ctx, xall, cown, wo, wi, w2, vec_full, bin_full)
    dq, dk, dk_send, dv, dv_send = attn_bwd(q, k, v, p, ctx, dctx)
    dkr, dvr = swap(dk_send, SWAP_C), swap(dv_send, SWAP_C)
    gx_a, gx_b, dwq, dwk, dwv, gv_proj = proj(xall, dq, dk, dkr, dv, dvr, gm1, wq, wk, wv)

    gv = jnp.concatenate([gv_proj[:2], gv_ffn[2:]], axis=0)
    grads = (dwq, dwk, dwv, dwo, dwi, dw2)
    by_owner = jnp.concatenate(
        [jnp.swapaxes(gv.reshape(8, fsdp, width), 0, 1), gbin.reshape(fsdp, 4, width)], axis=1
    )
    if direct:
        padded = jnp.pad(by_owner, ((0, 0), (0, 4), (0, 128 - width)))
        tot, output, grad_inputs, tvec = scatter_all(grads, out, gx_a, gx_b, padded, shards)
        tvec = tvec[:12, :width]
    else:
        tot = [
            lax.psum(lax.psum_scatter(g, "fsdp", scatter_dimension=0, tiled=True), "seq").astype(F32)
            for g in grads
        ]
        tvec = lax.psum(lax.psum_scatter(by_owner, "fsdp", scatter_dimension=0, tiled=True)[0], "seq")

        def joined(mine, other):
            here = lax.dynamic_update_slice_in_dim(
                jnp.zeros((pages_all, blk, d), mine.dtype), mine, x_at * pages, 0
            )
            return lax.dynamic_update_slice_in_dim(here, other, (1 - x_at) * pages, 0)

        output = joined(out[:, :blk], swap(out[:, blk:], SWAP_X))
        grad_inputs = joined(gx_a, swap(gx_b, SWAP_X).astype(F32))
    small = [tvec[i] for i in range(8)]
    g_bq, g_bv, g_bo, g_g1, g_s1, g_bo2, g_g2, g_s2 = small
    g_bi = tvec[8:].reshape(-1)
    t_q, t_k, t_v, t_o, t_i, t_2 = tot
    return (
        output, grad_inputs, t_q, g_bq, t_k, t_v, g_bv, t_o, g_bo, g_g1, g_s1,
        t_i, g_bi, t_2, g_bo2, g_g2, g_s2,
    )


def solution(mesh):
    vec, mat, act = P("fsdp"), P("fsdp", None), P("fsdp", "seq", None)
    return jax.shard_map(
        functools.partial(per_device, mesh.shape["fsdp"]),
        mesh=mesh,
        in_specs=(act, vec, mat, vec, mat, mat, vec, mat, vec, vec, vec, mat, vec, mat, vec, vec, vec, act),
        out_specs=(act, act, mat, vec, mat, mat, vec, mat, vec, vec, vec, mat, vec, mat, vec, vec, vec),
        check_vma=False,
    )
```

time: 399 us -> 315 us (0.79)
  Pallas kernels: 367 us -> 292 us
  local copies, waits for them, and re-layouts: 23.1 us -> 16.8 us
    pallas_call x2 -> x1, Pallas kernels: 158 us -> 102 us  [fwd(): call(fwd_body, (pages * 2 * d * d * (own + 2 * rows), sum((16 * w.size fo...]
    pallas_call x1, Pallas kernels: 60.2 us -> 41.7 us  [ffn(): call(ffn_body, (n * d * (12 * ff + 6 * d), 4 * d * ff * 2 + 12 * n * d *...]
    concatenate x1 -> x0, local copies, waits for them, and re-layouts: 6.11 us -> none  [per_device(): vec = jnp.concatenate(names + (b_inner,)).reshape(12, width)]
    unnamed x32 -> x30, local copies, waits for them, and re-layouts: 10.5 us -> 10.5 us
where the time goes in v2:
time: 315 us
  Pallas kernels  292 us (93%)
  local copies, waits for them, and re-layouts  16.8 us (5%)
    pallas_call x1, Pallas kernels, scatter_all(): call(scatter_body, (0, sum((16 * g.size for g in grads)), 0), in_specs=[A...  116 us
    pallas_call x1, Pallas kernels, fwd(): call(fwd_body, (pages * 2 * d * d * (own + 2 * rows), sum((16 * w.size fo...  102 us
    pallas_call x1, Pallas kernels, ffn(): call(ffn_body, (n * d * (12 * ff + 6 * d), 4 * d * ff * 2 + 12 * n * d *...  41.7 us
    pallas_call x1, Pallas kernels, attn_bwd(): call(attn_bwd_body, (pages * 10 * own * rows * d, pages * (own * rows * H...  19.7 us
    pallas_call x1, Pallas kernels, proj(): call(proj_body, (12 * n * d * d, 12 * d * d + 16 * n * d, 0), grid=(pages...  12.9 us
    unnamed x30, local copies, waits for them, and re-layouts  10.5 us
  transfers between devices with their start and end apart: 2, of which 2 were waited for; matrix products, arithmetic and copies ran while one was open for 0% of the time, Pallas kernels for 0%

profile of v2, /device:TPU:0, one launch (start us, length us, event | category | flops | bytes accessed | tf_op | source)
XLA Modules:
  0.0 314.9 jit_solution(11871394130912309975)
XLA Ops:
  0.7 1.2 reshape.149.refs_8_
  1.9 0.7 dynamic_slice.3
  2.6 0.1 add_multiply_fusion
  2.7 0.7 broadcast_subtract_fusion.thr
  3.4 101.9 %gather_attention.1 = (bf16[4,2,96,768]{3,2,1,0:T(8,128)(2,1)}, bf16[4,2,96,768]{3,2,1,0:T(8,128)(2,1)}, bf16[4,2,96,768]{3,2,1,0:T(8,128)(2,1)}, bf16[4,2,96,76...) custom-call(s32[3,4]{1,0:T(4,128)} %broadcast_subtract_fusion.thr, ...), custom_call_target="tpu_custom_call" | custom-call | flops 4529848320 | bytes 14155776 | tf_op jit(solution)/shard_map/gather_attention/pallas_call | solution.py:711
  105.3 41.7 %ffn.1 = (bf16[3,256,768]{2,1,0:T(8,128)(2,1)}, f32[3,256,768]{2,1,0:T(8,128)}, bf16[3,256,768]{2,1,0:T(8,128)(2,1)}, bf16[768,768]{1,0:T(8,128)(2,1)}, bf16[768...) custom-call(bf16[3,256,768]{2,1,0:T(8,128)(2,1)} %get-tuple-element.65.ctx, ...), custom_call_target="tpu_custom_call" | custom-call | flops 24461180928 | bytes 33030144 | tf_op jit(solution)/shard_map/ffn/pallas_call | solution.py:316
  147.0 0.0 copy-start.7
  147.0 0.0 copy-start.8
  147.0 19.7 %attn_bwd.1 = (bf16[3,256,768]{2,1,0:T(8,128)(2,1)}, bf16[3,256,768]{2,1,0:T(8,128)(2,1)}, bf16[3,256,768]{2,1,0:T(8,128)(2,1)}, bf16[3,256,768]{2,1,0:T(8,128)(2,1)}, bf16[3,256,768]{2,1,0:T(8,128)(2,1)}) custom-call(bf16[3,256,768]{2,1,0:T(8,128)(2,1)} %get-tuple-element.61.q, bf16[3,512,768]{2,1,0:T(8,128)(2,1)} %get-tuple-element.62.k, ...), custom_call_target="tpu_custom_call" | custom-call | flops 3019898880 | bytes 21233664 | tf_op jit(solution)/shard_map/attn_bwd/pallas_call | solution.py:169
  166.7 0.4 collective-permute-start
  167.1 0.1 collective-permute-start.1
  167.2 0.0 copy-done.7
  167.2 0.5 broadcast.27
  167.8 0.0 copy-done.8
  167.8 0.7 reduce.3
  168.4 0.1 reshape.163
  168.5 1.3 collective-permute-done.dkr
  169.8 0.0 copy-start.9
  169.8 1.7 collective-permute-done.1.dvr
  171.5 0.0 copy-start.10
  171.5 0.0 copy-done.9
  171.5 1.0 copy-done.10
  172.5 12.9 %proj_bwd.1 = (f32[3,128,768]{2,1,0:T(8,128)}, bf16[3,128,768]{2,1,0:T(8,128)(2,1)}, bf16[768,768]{1,0:T(8,128)(2,1)}, bf16[768,768]{1,0:T(8,128)(2,1)}, bf16[768,768]{1,0:T(8,128)(2,1)}, /*index=5*/f32[8,768]{1,0:T(8,128)}) custom-call(bf16[3,512,768]{2,1,0:T(8,128)(2,1)} %get-tuple-element.60.xall, bf16[3,256,768]{2,1,0:T(8,128)(2,1)} %get-tuple-element.73.dq, ...), custom_call_target="tpu_custom_call" | custom-call | flops 5435817984 | bytes 16515072 | tf_op jit(solution)/shard_map/proj_bwd/pallas_call | solution.py:385
  185.4 0.7 slice.43
  186.1 0.1 reshape.162
  186.2 0.6 select_maximum_fusion.gvec
  186.9 115.6 %scatter_all.1 = (f32[96,768]{1,0:T(8,128)}, f32[96,768]{1,0:T(8,128)}, f32[96,768]{1,0:T(8,128)}, f32[96,768]{1,0:T(8,128)}, f32[96,3072]{1,0:T(8,128)}, /*inde...) custom-call(bf16[4,2,96,768]{3,2,1,0:T(8,128)(2,1)} %bitcast.46, ...), custom_call_target="tpu_custom_call" | custom-call | bytes 113246208 | tf_op jit(solution)/shard_map/scatter_all/pallas_call | solution.py:927
  302.5 1.5 slice_bitcast_fusion
  304.0 0.7 slice.50
  304.7 0.7 reshape.164
  305.3 0.0 copy-start
  305.3 2.5 copy.46
  307.9 0.0 copy-done
  307.9 0.0 copy-start.6
  307.9 0.0 copy-start.5
  307.9 0.0 copy-start.4
  307.9 1.4 copy.47
  309.3 0.0 copy-done.6
  309.3 0.0 copy-start.3
  309.3 0.0 copy-start.2
  309.3 0.7 copy.48
  310.0 0.0 copy-done.5
  310.0 0.7 copy.49
  310.7 0.0 copy-done.4
  310.7 0.7 copy.50
  311.4 0.0 copy-done.3
  311.4 0.7 copy.51
  312.1 0.0 copy-done.2
  312.2 0.0 copy-start.1
  312.2 1.0 copy.52
  313.2 0.7 copy-done.1
  313.8 1.0 copy.53
  (3 shorter events, 0.0 us)
Async XLA Ops:
  147.0 20.2 %copy-start.7 = (f32[8,768]{1,0:T(8,128)S(1)}, f32[8,768]{1,0:T(8,128)}, u32[]{:S(2)}) copy-start(f32[8,768]{1,0:T(8,128)} %get-tuple-element.92) | copy-start | bytes 73732
  147.0 20.8 %copy-start.8 = (f32[1,3072]{1,0:T(1,128)S(1)}, f32[1,3072]{1,0:T(1,128)}, u32[]{:S(2)}) copy-start(f32[1,3072]{1,0:T(1,128)} %get-tuple-element.93) | copy-start | bytes 36868
  166.7 3.1 collective-permute-start
  167.1 4.4 %collective-permute-start.1 = (bf16[3,256,768]{2,1,0:T(8,128)(2,1)}, bf16[3,256,768]{2,1,0:T(8,128)(2,1)S(1)}, u32[]{:S(2)}, u32[]{:S(2)}) collective-permute-start(bf16[3,256,768]{2,1,0:T(8,128)(2,1)} %get-tuple-element.77), channel_id=1, source_target_pairs={{0,1},{1,0},{2,3},{3,2},{4,5},{5,4},{6,7},{7,6},{8,9},{9,8},{10,11... | collective-permute-start | bytes 3538952 | tf_op jit(solution)/shard_map/ppermute | solution.py:965
  169.8 1.7 copy-start.9
  171.5 1.0 copy-start.10
  305.3 2.5 copy-start
  307.9 1.4 copy-start.6
  307.9 2.1 copy-start.5
  307.9 2.9 copy-start.4
  309.3 2.2 copy-start.3
  309.3 2.9 copy-start.2
  312.2 1.7 copy-start.1
